TPU v7x, 512 devices: a whole 4x8x8 slice. The times are simulated.
512 devices in a mesh: blk: 128 (over x, y, z_lo, core), rep: 4 (over z_hi).
Axes of the slice: x: 4, y: 8, z: 8 (z_hi: 4, z_lo: 2; z = z_hi * 2 + z_lo), core: 2. Of those that a mesh axis runs over, the one named last changes fastest.
Arguments:
- image: bfloat16 [65536, 1024], P(('blk', 'rep')), may hold values from -100 to 100
- text: bfloat16 [65536, 1024], P(('blk', 'rep')), may hold values from -100 to 100
- positive: int32 [128, 512], P('blk', 'rep'), may hold values from 0 to 511, each once within a row
- logit_scale: float32 [1], replicated, may hold values from 85 to 270
Outputs:
- row_loss: float32 [65536], P(('blk', 'rep'))
- col_loss: float32 [65536], P(('blk', 'rep'))
- img_grad: float32 [65536, 1024], P(('blk', 'rep'))
- txt_grad: float32 [65536, 1024], P(('blk', 'rep'))
Inputs may be any that keep to these rules, and one draw needn't show every extreme that they name: Each row of positive names every index of its block once.
All inputs are finite; a program needn't handle non-finite values.
Results may differ from a plain program's by a relative error of at most 0.0081.
The roundings to bfloat16 on the way count: a program that leaves them out, or rounds other values in their place, can miss the bound.
Values may be sent and summed in bfloat16 or wider, within the bound.
A program may use at most 64 MiB of HBM per device.

v0:
```python
import jax
import jax.numpy as jnp
from jax import lax
from jax.sharding import PartitionSpec as P

STEPS = 4


def from_everyone(array, axis):
    count = lax.axis_size(axis)
    return lax.all_to_all(
        jnp.broadcast_to(array[None], (count, *array.shape)), axis, 0, 0, tiled=True
    )


def joined_along(blocks, dim):
    blocks = jnp.moveaxis(blocks, 0, dim)
    dims = blocks.shape
    return blocks.reshape(*dims[:dim], dims[dim] * dims[dim + 1], *dims[dim + 2 :])


def collect(array, axis, dim):
    blocks = from_everyone(array, axis)
    return joined_along(blocks, dim)


def passed_along(array, axis, by):
    count = lax.axis_size(axis)
    return lax.ppermute(array, axis, [(i, (i + by) % count) for i in range(count)])


def gathered_once(array, axis):
    leaves = jax.tree.leaves(array)
    sequence = sorted(range(len(leaves)), key=lambda k: -leaves[k].size)
    width = (1, *leaves[sequence[0]].shape)[-1]
    lines = [
        jnp.pad(leaves[k].reshape(-1), (0, -leaves[k].size % width)).reshape(-1, width)
        for k in sequence
    ]
    both, at, found = (from_everyone(jnp.concatenate(lines), axis), 0, {})
    for k, line in zip(sequence, lines):
        piece = both[:, at : at + len(line)].reshape(len(both), -1)
        found[k] = piece[:, : leaves[k].size].reshape(-1, *leaves[k].shape)
        at += len(line)
    numbers = iter(range(len(leaves)))
    return jax.tree.map(lambda _: found[next(numbers)], array)


def joined_by_halves(pieces, combine):
    while len(jax.tree.leaves(pieces)[0]) > 1:
        pieces = jax.vmap(combine)(
            *(jax.tree.map(lambda part: part[side::2], pieces) for side in (0, 1))
        )
    return jax.tree.map(lambda part: part[0], pieces)


def merged(array, axis, combine):
    pieces = gathered_once(array, axis)
    return joined_by_halves(pieces, combine)


def cut_along(array, dim, count):
    before, after = (array.shape[:dim], array.shape[dim + 1 :])
    return jnp.moveaxis(array.reshape(*before, count, -1, *after), dim, 0)


def sent_and_summed(array, axis, dim):
    count = lax.axis_size(axis)
    blocks = lax.all_to_all(cut_along(array, dim, count), axis, 0, 0, tiled=True)
    return jnp.sum(blocks.astype(jnp.float32), axis=0)


def normalize(values):
    widened = values.astype(jnp.float32)
    inverse = lax.rsqrt(jnp.sum(widened * widened, axis=-1, keepdims=True) + 1e-06)
    return (widened * inverse, inverse)


def combine_stats(earlier, later):
    highest = jnp.maximum(earlier[0], later[0])
    summed = earlier[1] * jnp.exp(earlier[0] - highest) + later[1] * jnp.exp(later[0] - highest)
    return (highest, summed, earlier[2] + later[2])


def tile_scores(img_part, text_tile, factor):
    return factor * jnp.einsum("id,jd->ij", img_part, text_tile, preferred_element_type=jnp.float32)


def tile_weights(img_part, text_tile, factor, row_lse, col_lse, onehot):
    scores = tile_scores(img_part, text_tile, factor)
    weight = 0.5 * (jnp.exp(scores - row_lse[:, None]) + jnp.exp(scores - col_lse[None, :]))
    if onehot is not None:
        weight = weight - onehot
    return weight.astype(jnp.bfloat16)


def on_device(image, text, positive, logit_scale):
    factor = logit_scale[0]
    row_count = image.shape[0]
    width = image.shape[1]
    quarter = lax.axis_index("rep")
    img_unit, img_inverse = normalize(image)
    txt_unit, txt_inverse = normalize(text)
    img_tile = img_unit.astype(jnp.bfloat16)
    txt_own = txt_unit.astype(jnp.bfloat16)
    home_tile = collect(txt_own, "rep", 0)
    block_rows = home_tile.shape[0]
    columns = lax.broadcasted_iota(jnp.int32, (row_count, block_rows), 1)
    onehot = (positive[0][:, None] == columns).astype(jnp.float32)
    kept = []
    moving = img_tile
    for loop_step in range(STEPS):
        if loop_step > 0:
            moving = passed_along(moving, "blk", -1)
            row_max, row_sum = passed_along((row_max, row_sum), "blk", -1)
        kept.append(moving)
        scores = tile_scores(moving, home_tile, factor)
        row_peak = jnp.max(scores, axis=1)
        col_peak = jnp.max(scores, axis=0)
        col_part = jnp.sum(jnp.exp(scores - col_peak[None, :]), axis=0)
        if loop_step == 0:
            row_max = row_peak
            row_sum = jnp.sum(jnp.exp(scores - row_peak[:, None]), axis=1)
            row_pos = jnp.sum(onehot * scores, axis=1)
            col_max, col_sum, col_pos = (col_peak, col_part, jnp.sum(onehot * scores, axis=0))
        else:
            highest = jnp.maximum(row_max, row_peak)
            row_sum = row_sum * jnp.exp(row_max - highest) + jnp.sum(
                jnp.exp(scores - highest[:, None]), axis=1
            )
            row_max = highest
            col_max, col_sum, col_pos = combine_stats(
                (col_max, col_sum, col_pos), (col_peak, col_part, jnp.zeros_like(col_peak))
            )
    col_max, col_sum, col_pos = merged((col_max, col_sum, col_pos), "rep", combine_stats)
    col_lse = col_max + jnp.log(col_sum)
    row_lse = row_max + jnp.log(row_sum)
    travel = (row_lse, jnp.zeros((row_count, width), jnp.float32))
    text_terms = jnp.zeros((block_rows, width), jnp.float32)
    for loop_step in range(STEPS - 1, -1, -1):
        if loop_step < STEPS - 1:
            travel = passed_along((travel[0], travel[1]), "blk", 1)
        tile = kept[loop_step]
        weight = tile_weights(
            tile, home_tile, factor, travel[0], col_lse, onehot if loop_step == 0 else None
        )
        travel = (
            travel[0],
            travel[1] + jnp.dot(weight, home_tile, preferred_element_type=jnp.float32),
        )
        text_terms = text_terms + jnp.einsum(
            "ij,id->jd", weight, tile, preferred_element_type=jnp.float32
        )
    row_lse, img_acc = travel
    col_lse_home, col_pos_home = (col_lse, col_pos)
    row_loss = row_lse - row_pos
    text_share = sent_and_summed(text_terms.astype(jnp.bfloat16), "rep", 0)
    img_sum = factor * img_acc
    txt_sum = factor * text_share
    img_grad = (
        img_sum - img_unit * jnp.sum(img_unit * img_sum, axis=-1, keepdims=True)
    ) * img_inverse
    txt_grad = (
        txt_sum - txt_unit * jnp.sum(txt_unit * txt_sum, axis=-1, keepdims=True)
    ) * txt_inverse
    col_whole = col_lse_home - col_pos_home
    col_loss = lax.dynamic_slice_in_dim(col_whole, quarter * row_count, row_count)
    return (row_loss, col_loss, img_grad, txt_grad)


def solution(mesh):
    placed = (P(("blk", "rep"), None), P(("blk", "rep"), None), P("blk", "rep"), P())
    return jax.shard_map(
        on_device,
        mesh=mesh,
        in_specs=placed,
        out_specs=(
            P(("blk", "rep")),
            P(("blk", "rep")),
            P(("blk", "rep"), None),
            P(("blk", "rep"), None),
        ),
        check_vma=False,
    )
```

profile of v0, /device:TPU:128, one launch (start us, length us, event | category | flops | bytes accessed | tf_op | source)
XLA Modules:
  0.0 166.4 jit_solution(11698450292557008222)
XLA Ops:
  4.0 9.2 %all-to-all-start = ((bf16[4,128,1024]{2,1,0:T(8,128)(2,1)}), bf16[4,128,1024]{2,1,0:T(8,128)(2,1)S(1)}, u32[]{:S(2)}, u32[]{:S(2)}) async-start(bf16[4,128,1024]{2,1,0:T(8,128)(2,1)} %broadcast_in_dim.4), calls=%async_computation | async-start | bytes 2097152 | tf_op jit(solution)/shard_map/all_to_all | solution.py:11
  13.4 7.4 %collective-permute-start.1 = (bf16[128,1024]{1,0:T(8,128)(2,1)S(1)}, bf16[128,1024]{1,0:T(8,128)(2,1)S(1)}, u32[]{:S(2)}, u32[]{:S(2)}) collective-permute-start(bf16[128,1024]{1,0:T(8,128)(2,1)S(1)} %fusion.5), channel_id=1, source_target_pairs={{0,508},{4,0},{8,4},{12,8},{16,12},{20,16},{24,20},{28,24},{32,28}... | collective-permute-start | bytes 786440 | tf_op jit(solution)/shard_map/ppermute | solution.py:29
  20.8 4.2 %collective-permute-done.1 = bf16[128,1024]{1,0:T(8,128)(2,1)S(1)} collective-permute-done((bf16[128,1024]{1,0:T(8,128)(2,1)S(1)}, bf16[128,1024]{1,0:T(8,128)(2,1)S(1)}, u32[]{:S(2)}, u32[]{:S(2)}) %collective-permute-start.1) | collective-permute-done | bytes 262176 | tf_op jit(solution)/shard_map/ppermute | solution.py:29
  25.0 9.5 %collective-permute-start.3 = (bf16[128,1024]{1,0:T(8,128)(2,1)S(1)}, bf16[128,1024]{1,0:T(8,128)(2,1)S(1)}, u32[]{:S(2)}, u32[]{:S(2)}) collective-permute-start(bf16[128,1024]{1,0:T(8,128)(2,1)S(1)} %collective-permute-done.1), channel_id=1, source_target_pairs={{0,508},{4,0},{8,4},{12,8},{16,12},{20,16},{24,20},{28,24},{32,28}... | collective-permute-start | bytes 786440 | tf_op jit(solution)/shard_map/ppermute | solution.py:29
  35.2 8.2 %collective-permute-done.3 = bf16[128,1024]{1,0:T(8,128)(2,1)S(1)} collective-permute-done((bf16[128,1024]{1,0:T(8,128)(2,1)S(1)}, bf16[128,1024]{1,0:T(8,128)(2,1)S(1)}, u32[]{:S(2)}, u32[]{:S(2)}) %collective-permute-start.3) | collective-permute-done | bytes 262176 | tf_op jit(solution)/shard_map/ppermute | solution.py:29
  43.4 6.7 %collective-permute-start.5 = (bf16[128,1024]{1,0:T(8,128)(2,1)S(1)}, bf16[128,1024]{1,0:T(8,128)(2,1)S(1)}, u32[]{:S(2)}, u32[]{:S(2)}) collective-permute-start(bf16[128,1024]{1,0:T(8,128)(2,1)S(1)} %collective-permute-done.3), channel_id=1, source_target_pairs={{0,508},{4,0},{8,4},{12,8},{16,12},{20,16},{24,20},{28,24},{32,28}... | collective-permute-start | bytes 786440 | tf_op jit(solution)/shard_map/ppermute | solution.py:29
  50.7 6.8 %collective-permute-start = (f32[128]{0:T(128)S(1)}, f32[128]{0:T(128)S(1)}, u32[]{:S(2)}, u32[]{:S(2)}) collective-permute-start(f32[128]{0:T(128)S(1)} %get-tuple-element.32), channel_id=1, source_target_pairs={{0,508},{4,0},{8,4},{12,8},{16,12},{20,16},{24,20},{28,24},{32,28}... | collective-permute-start | bytes 1544 | tf_op jit(solution)/shard_map/ppermute | solution.py:29
  57.7 3.8 %collective-permute-start.6 = (f32[128]{0:T(128)S(1)}, f32[128]{0:T(128)S(1)}, u32[]{:S(2)}, u32[]{:S(2)}) collective-permute-start(f32[128]{0:T(128)S(1)} %get-tuple-element.16), channel_id=1, source_target_pairs={{0,508},{4,0},{8,4},{12,8},{16,12},{20,16},{24,20},{28,24},{32,28}... | collective-permute-start | bytes 1544 | tf_op jit(solution)/shard_map/ppermute | solution.py:29
  63.5 3.1 %collective-permute-start.2 = (f32[128]{0:T(128)S(1)}, f32[128]{0:T(128)S(1)}, u32[]{:S(2)}, u32[]{:S(2)}) collective-permute-start(f32[128]{0:T(128)S(1)} %max.57), channel_id=1, source_target_pairs={{0,508},{4,0},{8,4},{12,8},{16,12},{20,16},{24,20},{28,24},{32,28}... | collective-permute-start | bytes 1544 | tf_op jit(solution)/shard_map/ppermute | solution.py:29
  66.8 3.8 %collective-permute-start.7 = (f32[128]{0:T(128)S(1)}, f32[128]{0:T(128)S(1)}, u32[]{:S(2)}, u32[]{:S(2)}) collective-permute-start(f32[128]{0:T(128)S(1)} %multiply_add_fusion.3), channel_id=1, source_target_pairs={{0,508},{4,0},{8,4},{12,8},{16,12},{20,16},{24,20},{28,24},{32,28}... | collective-permute-start | bytes 1544 | tf_op jit(solution)/shard_map/ppermute | solution.py:29
  70.7 5.0 %collective-permute-start.4 = (f32[128]{0:T(128)S(1)}, f32[128]{0:T(128)S(1)}, u32[]{:S(2)}, u32[]{:S(2)}) collective-permute-start(f32[128]{0:T(128)S(1)} %max.58), channel_id=1, source_target_pairs={{0,508},{4,0},{8,4},{12,8},{16,12},{20,16},{24,20},{28,24},{32,28}... | collective-permute-start | bytes 1544 | tf_op jit(solution)/shard_map/ppermute | solution.py:29
  75.9 3.8 %collective-permute-start.8 = (f32[128]{0:T(128)S(1)}, f32[128]{0:T(128)S(1)}, u32[]{:S(2)}, u32[]{:S(2)}) collective-permute-start(f32[128]{0:T(128)S(1)} %multiply_add_fusion.2), channel_id=1, source_target_pairs={{0,508},{4,0},{8,4},{12,8},{16,12},{20,16},{24,20},{28,24},{32,28}... | collective-permute-start | bytes 1544 | tf_op jit(solution)/shard_map/ppermute | solution.py:29
  80.6 6.0 %all-to-all-start.1 = ((f32[4,3,512]{2,1,0:T(4,128)}), f32[4,3,512]{2,1,0:T(4,128)S(1)}, u32[]{:S(2)}, u32[]{:S(2)}) async-start(f32[4,3,512]{2,1,0:T(4,128)} %broadcast_in_dim.5), calls=%async_computation.1 | async-start | bytes 65536 | tf_op jit(solution)/shard_map/all_to_all | solution.py:11
  88.6 7.2 %collective-permute-done.9 = f32[128]{0:T(128)S(1)} collective-permute-done((f32[128]{0:T(128)S(1)}, f32[128]{0:T(128)S(1)}, u32[]{:S(2)}, u32[]{:S(2)}) %collective-permute-start.9) | collective-permute-done | bytes 544 | tf_op jit(solution)/shard_map/ppermute | solution.py:29
  97.7 7.2 %collective-permute-done.10 = f32[128]{0:T(128)S(1)} collective-permute-done((f32[128]{0:T(128)S(1)}, f32[128]{0:T(128)S(1)}, u32[]{:S(2)}, u32[]{:S(2)}) %collective-permute-start.10) | collective-permute-done | bytes 544 | tf_op jit(solution)/shard_map/ppermute | solution.py:29
  111.2 2.8 %collective-permute-done.11 = f32[128]{0:T(128)S(1)} collective-permute-done((f32[128]{0:T(128)S(1)}, f32[128]{0:T(128)S(1)}, u32[]{:S(2)}, u32[]{:S(2)}) %collective-permute-start.11) | collective-permute-done | bytes 544 | tf_op jit(solution)/shard_map/ppermute | solution.py:29
  116.1 7.2 %all-to-all-start.2 = ((bf16[4,128,1024]{2,1,0:T(8,128)(2,1)}), bf16[4,128,1024]{2,1,0:T(8,128)(2,1)S(1)}, u32[]{:S(2)}, u32[]{:S(2)}) async-start(bf16[4,128,1024]{2,1,0:T(8,128)(2,1)} %bitcast.16), calls=%async_computation.2 | async-start | bytes 2097152 | tf_op jit(solution)/shard_map/all_to_all | solution.py:69
  123.3 3.5 %collective-permute-done.12 = f32[128,1024]{1,0:T(8,128)} collective-permute-done((f32[128,1024]{1,0:T(8,128)}, f32[128,1024]{1,0:T(8,128)}, u32[]{:S(2)}, u32[]{:S(2)}) %collective-permute-start.12) | collective-permute-done | bytes 524320 | tf_op jit(solution)/shard_map/ppermute | solution.py:29
  126.7 2.2 %convolution_add_fusion = f32[128,1024]{1,0:T(8,128)} fusion(f32[128,1024]{1,0:T(8,128)} %collective-permute-done.12, bf16[512,1024]{1,0:T(8,128)(2,1)S(1)} %bitcast.52, f32[128,512]{1,0:T(8,128)S(1)} %get-tuple-element.35, f32[128]{0:T(128)S(1)} %collective-permute-done.9, f32[512]{0:T(512)S(1)} %bitcast.60), kind=kOutput, calls=%fused_computation.2 | convolution fusion | flops 134676480 | bytes 2361856 | tf_op jit(solution)/shard_map/dot_general | solution.py:149
  129.0 2.0 %collective-permute-start.13 = (f32[128,1024]{1,0:T(8,128)}, f32[128,1024]{1,0:T(8,128)}, u32[]{:S(2)}, u32[]{:S(2)}) collective-permute-start(f32[128,1024]{1,0:T(8,128)} %convolution_add_fusion), channel_id=1, source_target_pairs={{0,4},{4,8},{8,12},{12,16},{16,20},{20,24},{24,28},{28,32},{32,36}... | collective-permute-start | bytes 1572872 | tf_op jit(solution)/shard_map/ppermute | solution.py:29
  132.1 13.5 %collective-permute-done.13 = f32[128,1024]{1,0:T(8,128)} collective-permute-done((f32[128,1024]{1,0:T(8,128)}, f32[128,1024]{1,0:T(8,128)}, u32[]{:S(2)}, u32[]{:S(2)}) %collective-permute-start.13) | collective-permute-done | bytes 524320 | tf_op jit(solution)/shard_map/ppermute | solution.py:29
  145.6 2.2 %fusion.26 = f32[128,1024]{1,0:T(8,128)} fusion(f32[128,1024]{1,0:T(8,128)} %collective-permute-done.13, bf16[512,1024]{1,0:T(8,128)(2,1)S(1)} %bitcast.53, f32[128,512]{1,0:T(8,128)S(1)} %get-tuple-element.34, f32[128]{0:T(128)S(1)} %collective-permute-done.10, f32[512]{0:T(512)S(1)} %bitcast.61), kind=kOutput, calls=%fused_computation.69 | convolution fusion | flops 134676480 | bytes 2361856 | tf_op jit(solution)/shard_map/dot_general | solution.py:149
  151.2 11.7 %collective-permute-done.14 = f32[128,1024]{1,0:T(8,128)} collective-permute-done((f32[128,1024]{1,0:T(8,128)}, f32[128,1024]{1,0:T(8,128)}, u32[]{:S(2)}, u32[]{:S(2)}) %collective-permute-start.14) | collective-permute-done | bytes 524320 | tf_op jit(solution)/shard_map/ppermute | solution.py:29
  164.4 2.1 %fusion.8 = f32[128,1024]{1,0:T(8,128)} fusion(bf16[128,1024]{1,0:T(8,128)(2,1)S(1)} %copy-done.1, f32[128]{0:T(128)S(1)} %get-tuple-element.37, f32[128]{0:T(128)S(1)} %add_rsqrt_fusion.1, f32[128,1024]{1,0:T(8,128)} %collective-permute-done.14, f32[128,1024]{1,0:T(8,128)S(1)} %get-tuple-element.38, f32[]{:T(128)} %bitcast.43), kind=kLoop, calls=%fused_computation.19 | loop fusion | flops 917504 | bytes 1836036 | tf_op jit(solution)/shard_map/mul | solution.py:160
  (71 shorter events, 25.7 us)
Async XLA Ops:
  0.6 12.5 %copy-start.1 = (bf16[128,1024]{1,0:T(8,128)(2,1)S(1)}, bf16[128,1024]{1,0:T(8,128)(2,1)}, u32[]{:S(2)}) copy-start(bf16[128,1024]{1,0:T(8,128)(2,1)} %param.4) | copy-start | bytes 786436
  4.0 57.6 %copy-start.2 = (s32[1,128]{1,0:T(1,128)S(1)}, s32[1,128]{1,0:T(1,128)}, u32[]{:S(2)}) copy-start(s32[1,128]{1,0:T(1,128)} %param.6) | copy-start | bytes 1540
  4.0 46.1 %all-to-all-start = ((bf16[4,128,1024]{2,1,0:T(8,128)(2,1)}), bf16[4,128,1024]{2,1,0:T(8,128)(2,1)S(1)}, u32[]{:S(2)}, u32[]{:S(2)}) async-start(bf16[4,128,1024]{2,1,0:T(8,128)(2,1)} %broadcast_in_dim.4), calls=%async_computation | async-start | bytes 2097152 | tf_op jit(solution)/shard_map/all_to_all | solution.py:11
  13.4 11.6 %collective-permute-start.1 = (bf16[128,1024]{1,0:T(8,128)(2,1)S(1)}, bf16[128,1024]{1,0:T(8,128)(2,1)S(1)}, u32[]{:S(2)}, u32[]{:S(2)}) collective-permute-start(bf16[128,1024]{1,0:T(8,128)(2,1)S(1)} %fusion.5), channel_id=1, source_target_pairs={{0,508},{4,0},{8,4},{12,8},{16,12},{20,16},{24,20},{28,24},{32,28}... | collective-permute-start | bytes 786440 | tf_op jit(solution)/shard_map/ppermute | solution.py:29
  25.0 18.4 %collective-permute-start.3 = (bf16[128,1024]{1,0:T(8,128)(2,1)S(1)}, bf16[128,1024]{1,0:T(8,128)(2,1)S(1)}, u32[]{:S(2)}, u32[]{:S(2)}) collective-permute-start(bf16[128,1024]{1,0:T(8,128)(2,1)S(1)} %collective-permute-done.1), channel_id=1, source_target_pairs={{0,508},{4,0},{8,4},{12,8},{16,12},{20,16},{24,20},{28,24},{32,28}... | collective-permute-start | bytes 786440 | tf_op jit(solution)/shard_map/ppermute | solution.py:29
  43.4 19.5 %collective-permute-start.5 = (bf16[128,1024]{1,0:T(8,128)(2,1)S(1)}, bf16[128,1024]{1,0:T(8,128)(2,1)S(1)}, u32[]{:S(2)}, u32[]{:S(2)}) collective-permute-start(bf16[128,1024]{1,0:T(8,128)(2,1)S(1)} %collective-permute-done.3), channel_id=1, source_target_pairs={{0,508},{4,0},{8,4},{12,8},{16,12},{20,16},{24,20},{28,24},{32,28}... | collective-permute-start | bytes 786440 | tf_op jit(solution)/shard_map/ppermute | solution.py:29
  50.7 12.8 %collective-permute-start = (f32[128]{0:T(128)S(1)}, f32[128]{0:T(128)S(1)}, u32[]{:S(2)}, u32[]{:S(2)}) collective-permute-start(f32[128]{0:T(128)S(1)} %get-tuple-element.32), channel_id=1, source_target_pairs={{0,508},{4,0},{8,4},{12,8},{16,12},{20,16},{24,20},{28,24},{32,28}... | collective-permute-start | bytes 1544 | tf_op jit(solution)/shard_map/ppermute | solution.py:29
  57.7 9.1 %collective-permute-start.6 = (f32[128]{0:T(128)S(1)}, f32[128]{0:T(128)S(1)}, u32[]{:S(2)}, u32[]{:S(2)}) collective-permute-start(f32[128]{0:T(128)S(1)} %get-tuple-element.16), channel_id=1, source_target_pairs={{0,508},{4,0},{8,4},{12,8},{16,12},{20,16},{24,20},{28,24},{32,28}... | collective-permute-start | bytes 1544 | tf_op jit(solution)/shard_map/ppermute | solution.py:29
  63.5 7.1 %collective-permute-start.2 = (f32[128]{0:T(128)S(1)}, f32[128]{0:T(128)S(1)}, u32[]{:S(2)}, u32[]{:S(2)}) collective-permute-start(f32[128]{0:T(128)S(1)} %max.57), channel_id=1, source_target_pairs={{0,508},{4,0},{8,4},{12,8},{16,12},{20,16},{24,20},{28,24},{32,28}... | collective-permute-start | bytes 1544 | tf_op jit(solution)/shard_map/ppermute | solution.py:29
  66.8 9.1 %collective-permute-start.7 = (f32[128]{0:T(128)S(1)}, f32[128]{0:T(128)S(1)}, u32[]{:S(2)}, u32[]{:S(2)}) collective-permute-start(f32[128]{0:T(128)S(1)} %multiply_add_fusion.3), channel_id=1, source_target_pairs={{0,508},{4,0},{8,4},{12,8},{16,12},{20,16},{24,20},{28,24},{32,28}... | collective-permute-start | bytes 1544 | tf_op jit(solution)/shard_map/ppermute | solution.py:29
  70.7 9.1 %collective-permute-start.4 = (f32[128]{0:T(128)S(1)}, f32[128]{0:T(128)S(1)}, u32[]{:S(2)}, u32[]{:S(2)}) collective-permute-start(f32[128]{0:T(128)S(1)} %max.58), channel_id=1, source_target_pairs={{0,508},{4,0},{8,4},{12,8},{16,12},{20,16},{24,20},{28,24},{32,28}... | collective-permute-start | bytes 1544 | tf_op jit(solution)/shard_map/ppermute | solution.py:29
  75.9 10.7 %collective-permute-start.8 = (f32[128]{0:T(128)S(1)}, f32[128]{0:T(128)S(1)}, u32[]{:S(2)}, u32[]{:S(2)}) collective-permute-start(f32[128]{0:T(128)S(1)} %multiply_add_fusion.2), channel_id=1, source_target_pairs={{0,508},{4,0},{8,4},{12,8},{16,12},{20,16},{24,20},{28,24},{32,28}... | collective-permute-start | bytes 1544 | tf_op jit(solution)/shard_map/ppermute | solution.py:29
  80.6 26.2 %all-to-all-start.1 = ((f32[4,3,512]{2,1,0:T(4,128)}), f32[4,3,512]{2,1,0:T(4,128)S(1)}, u32[]{:S(2)}, u32[]{:S(2)}) async-start(f32[4,3,512]{2,1,0:T(4,128)} %broadcast_in_dim.5), calls=%async_computation.1 | async-start | bytes 65536 | tf_op jit(solution)/shard_map/all_to_all | solution.py:11
  86.7 9.1 %collective-permute-start.9 = (f32[128]{0:T(128)S(1)}, f32[128]{0:T(128)S(1)}, u32[]{:S(2)}, u32[]{:S(2)}) collective-permute-start(f32[128]{0:T(128)S(1)} %log_add_fusion.1), channel_id=1, source_target_pairs={{0,4},{4,8},{8,12},{12,16},{16,20},{20,24},{24,28},{28,32},{32,36}... | collective-permute-start | bytes 1544 | tf_op jit(solution)/shard_map/ppermute | solution.py:29
  95.8 9.1 %collective-permute-start.10 = (f32[128]{0:T(128)S(1)}, f32[128]{0:T(128)S(1)}, u32[]{:S(2)}, u32[]{:S(2)}) collective-permute-start(f32[128]{0:T(128)S(1)} %collective-permute-done.9), channel_id=1, source_target_pairs={{0,4},{4,8},{8,12},{12,16},{16,20},{20,24},{24,28},{28,32},{32,36}... | collective-permute-start | bytes 1544 | tf_op jit(solution)/shard_map/ppermute | solution.py:29
  104.9 9.1 %collective-permute-start.11 = (f32[128]{0:T(128)S(1)}, f32[128]{0:T(128)S(1)}, u32[]{:S(2)}, u32[]{:S(2)}) collective-permute-start(f32[128]{0:T(128)S(1)} %collective-permute-done.10), channel_id=1, source_target_pairs={{0,4},{4,8},{8,12},{12,16},{16,20},{20,24},{24,28},{28,32},{32,36}... | collective-permute-start | bytes 1544 | tf_op jit(solution)/shard_map/ppermute | solution.py:29
  108.2 18.6 %collective-permute-start.12 = (f32[128,1024]{1,0:T(8,128)}, f32[128,1024]{1,0:T(8,128)}, u32[]{:S(2)}, u32[]{:S(2)}) collective-permute-start(f32[128,1024]{1,0:T(8,128)} %fusion.22), channel_id=1, source_target_pairs={{0,4},{4,8},{8,12},{12,16},{16,20},{20,24},{24,28},{28,32},{32,36}... | collective-permute-start | bytes 1572872 | tf_op jit(solution)/shard_map/ppermute | solution.py:29
  116.1 33.7 %all-to-all-start.2 = ((bf16[4,128,1024]{2,1,0:T(8,128)(2,1)}), bf16[4,128,1024]{2,1,0:T(8,128)(2,1)S(1)}, u32[]{:S(2)}, u32[]{:S(2)}) async-start(bf16[4,128,1024]{2,1,0:T(8,128)(2,1)} %bitcast.16), calls=%async_computation.2 | async-start | bytes 2097152 | tf_op jit(solution)/shard_map/all_to_all | solution.py:69
  129.0 21.0 %copy-start = (bf16[128,1024]{1,0:T(8,128)(2,1)S(1)}, bf16[128,1024]{1,0:T(8,128)(2,1)}, u32[]{:S(2)}) copy-start(bf16[128,1024]{1,0:T(8,128)(2,1)} %param.5) | copy-start | bytes 786436
  129.0 16.6 %collective-permute-start.13 = (f32[128,1024]{1,0:T(8,128)}, f32[128,1024]{1,0:T(8,128)}, u32[]{:S(2)}, u32[]{:S(2)}) collective-permute-start(f32[128,1024]{1,0:T(8,128)} %convolution_add_fusion), channel_id=1, source_target_pairs={{0,4},{4,8},{8,12},{12,16},{16,20},{20,24},{24,28},{28,32},{32,36}... | collective-permute-start | bytes 1572872 | tf_op jit(solution)/shard_map/ppermute | solution.py:29
  147.8 15.0 %collective-permute-start.14 = (f32[128,1024]{1,0:T(8,128)}, f32[128,1024]{1,0:T(8,128)}, u32[]{:S(2)}, u32[]{:S(2)}) collective-permute-start(f32[128,1024]{1,0:T(8,128)} %fusion.26), channel_id=1, source_target_pairs={{0,4},{4,8},{8,12},{12,16},{16,20},{20,24},{24,28},{28,32},{32,36}... | collective-permute-start | bytes 1572872 | tf_op jit(solution)/shard_map/ppermute | solution.py:29
where the time goes:
time: 167 us; the launch traced here: 166 us
  starting transfers between devices  83.9 us (50%)
  waiting for transfers between devices  58.2 us (35%)
  matrix products  12.6 us (8%)
  other arithmetic  8.09 us (5%)
  local copies, waits for them, and re-layouts  1.95 us (1%)
    ppermute x15, starting transfers between devices, passed_along(): lax.ppermute(array, axis, [(i, (i + by) % count) for i in range(count)])  61.6 us
    ppermute x15, waiting for transfers between devices, passed_along(): lax.ppermute(array, axis, [(i, (i + by) % count) for i in range(count)])  58.2 us
    all_to_all x2, starting transfers between devices, from_everyone(): lax.all_to_all(jnp.broadcast_to(array[None], (count, *array.shape)), axis...  15.2 us
    all_to_all x1, starting transfers between devices, sent_and_summed(): lax.all_to_all(cut_along(array, dim, count), axis, 0, 0, tiled=True)  7.19 us
    dot_general x4, matrix products, on_device(): jnp.dot(weight, home_tile, preferred_element_type=jnp.float32)  7.14 us
  transfers between devices with their start and end apart: 18, of which 8 were waited for; matrix products, arithmetic and copies ran while one was open for 9% of the time, Pallas kernels for 0%

commit v1 on v0

v1 whole, which is shorter than its diff:
```python
import functools

import jax
import jax.numpy as jnp
from jax import lax
from jax.experimental import pallas as pl
from jax.experimental.pallas import tpu as pltpu
from jax.sharding import PartitionSpec as P

MESH = pl.DeviceIdType.MESH
F32 = jnp.float32
BF16 = jnp.bfloat16
ROWS = 128
HALF = 64
RING = 8
LOW = -1e30


def unit_of(values):
    widened = values.astype(F32)
    inverse = lax.rsqrt(jnp.sum(widened * widened, axis=-1, keepdims=True) + 1e-06)
    return widened * inverse, inverse


def dot(a, b, dims):
    return lax.dot_general(a, b, (dims, ((), ())), preferred_element_type=F32)


def kernel(
    columns,
    scale_ref, img_ref, txt_ref, pos_ref,
    row_ref, col_ref, igrad_ref, tgrad_ref,
    texts, images, scores, weights, terms, img_acc,
    peak, part, row_hit,
    row_stat, row_got, col_stat, col_got, row_lse, col_lse, row_wide,
    sums_out, sums_in, img_out, img_in,
    txt_send, txt_recv, pic_send, pic_recv, rs_send, rs_recv, cs_send, cs_recv,
    sum_send, sum_recv, ig_send, ig_recv,
):
    blk, rep = lax.axis_index("blk"), lax.axis_index("rep")
    core = lax.rem(blk, 2)
    odd = lax.rem(lax.div(blk, 2), 2)
    col = lax.div(blk, 4)
    z = 2 * rep + odd
    factor = scale_ref[0]

    def device(column, height, which):
        return (4 * column + 2 * lax.rem(height, 2) + which, lax.div(height, 2))

    def ring(by):
        return lax.rem(z + by + RING, RING)

    def slot(height):
        return 4 * lax.rem(height, 2) + lax.div(height, 2)

    up, down = lax.rem(col + 1, columns), lax.rem(col + columns - 1, columns)
    mate = device(col, z, 1 - core)
    ups = [device(up, z, c) for c in (0, 1)]
    downs = [device(down, z, c) for c in (0, 1)]
    rings = [device(col, ring(r), core) for r in range(1, RING)]

    barrier = pltpu.get_barrier_semaphore()
    friends = [mate, *ups, *downs, *rings]
    for friend in friends:
        pl.semaphore_signal(barrier, inc=1, device_id=friend, device_id_type=MESH)

    even_from = ROWS * core * (1 - odd)
    odd_from = jnp.where(odd == 0, 2 * ROWS, ROWS * core)
    starts = (
        pl.multiple_of(jnp.where(odd == 0, even_from, odd_from), ROWS),
        pl.multiple_of(jnp.where(odd == 0, odd_from, even_from), ROWS),
    )

    img_unit, _ = unit_of(img_ref[...])
    images[core] = img_unit.astype(BF16)
    txt_unit, _ = unit_of(txt_ref[...])
    texts[slot(z)] = txt_unit.astype(BF16)

    pl.semaphore_wait(barrier, len(friends))

    def text_copy(way, depth, half):
        place = slot(ring(-depth if way == 0 else depth))
        part_of = texts.at[place, pl.ds(half * HALF, HALF)]
        to = device(col, ring(1 if way == 0 else -1), core)
        return pltpu.make_async_remote_copy(
            src_ref=part_of, dst_ref=part_of,
            send_sem=txt_send.at[way, depth, half], recv_sem=txt_recv.at[way, depth, half],
            device_id=to, device_id_type=MESH,
        )

    def text_arrival(way, depth, half):
        place = slot(ring(-depth if way == 0 else depth))
        part_of = texts.at[place, pl.ds(half * HALF, HALF)]
        return pltpu.make_async_remote_copy(
            src_ref=part_of, dst_ref=part_of,
            send_sem=txt_send.at[way, depth - 1, half], recv_sem=txt_recv.at[way, depth - 1, half],
            device_id=mate, device_id_type=MESH,
        )

    sent = []

    def start(copy):
        copy.start()
        sent.append(copy)

    for half in (0, 1):
        start(text_copy(0, 0, half))
        start(text_copy(1, 0, 1 - half))

    def image_copy(which, to, there):
        return pltpu.make_async_remote_copy(
            src_ref=images.at[core], dst_ref=images.at[there],
            send_sem=pic_send.at[which], recv_sem=pic_recv.at[which],
            device_id=to, device_id_type=MESH,
        )

    def image_arrival(which, there):
        return pltpu.make_async_remote_copy(
            src_ref=images.at[there], dst_ref=images.at[there],
            send_sem=pic_send.at[which], recv_sem=pic_recv.at[which],
            device_id=mate, device_id_type=MESH,
        )

    start(image_copy(0, mate, core))
    start(image_copy(1, device(down, z, core), 2 + core))
    start(image_copy(2, device(down, z, 1 - core), 2 + core))

    positive = jnp.broadcast_to(pos_ref[...].astype(F32), (ROWS, ROWS)).T.astype(jnp.int32)
    lanes = lax.broadcasted_iota(jnp.int32, (ROWS, ROWS), 1)
    peak[...] = jnp.full(peak.shape, LOW, F32)
    part[...] = jnp.zeros(part.shape, F32)
    row_hit[...] = jnp.zeros(row_hit.shape, F32)
    col_stat[...] = jnp.zeros(col_stat.shape, F32)
    row_stat[0] = jnp.full((8, ROWS), LOW, F32)
    row_stat[1] = jnp.zeros((8, ROWS), F32)

    def number(step):
        return 2 * abs(step) - (1 if step < 0 or step == 4 else 0)

    def score(step):
        height = ring(step)
        kind = abs(step) % 2
        first = lax.div(starts[kind], ROWS)
        left = images[pl.ds(first, 2)].reshape(2 * ROWS, -1)
        value = factor * dot(left, texts[slot(height)], ((1,), (1,)))
        scores[number(step)] = value
        old = peak[kind]
        top = jnp.maximum(old, value)
        part[kind] = part[kind] * jnp.exp(old - top) + jnp.exp(value - top)
        peak[kind] = top
        highest = jnp.max(value, axis=0, keepdims=True)
        col_stat[0, pl.ds(height, 1), :] = highest
        col_stat[1, pl.ds(height, 1), :] = jnp.sum(jnp.exp(value - highest), axis=0, keepdims=True)
        if kind == 0:
            hit = jnp.where(hits(height), value[:ROWS], 0.0)
            row_hit[...] += hit
            col_stat[2, pl.ds(height, 1), :] = jnp.sum(hit, axis=0, keepdims=True)

    def hits(height):
        return positive == lanes + ROWS * lax.div(height, 2)

    def pass_on(depth):
        for turn in (0, 1):
            for way in (0, 1):
                half = turn if way == 0 else 1 - turn
                if depth < 4 or turn == 0:
                    text_arrival(way, depth, half).wait_recv()
                    if depth < 3 or (depth == 3 and turn == 0):
                        start(text_copy(way, depth, half))

    pass_on(1)
    pass_on(2)
    image_arrival(0, 1 - core).wait_recv()
    image_arrival(1, 2 + core).wait_recv()
    image_arrival(2, 3 - core).wait_recv()
    for step in (0, -1, 1, -2, 2):
        score(step)
    pass_on(3)
    score(-3)
    score(3)
    pass_on(4)
    score(4)

    for kind in (0, 1):
        for side in (0, 1):
            tops = peak[kind, side * ROWS : (side + 1) * ROWS, :].T
            parts = part[kind, side * ROWS : (side + 1) * ROWS, :].T
            top = jnp.max(tops, axis=0, keepdims=True)
            total = jnp.sum(parts * jnp.exp(tops - top), axis=0, keepdims=True)
            at = pl.ds(lax.div(starts[kind], ROWS) + side, 1)
            old_top, old_total = row_stat[0, at, :], row_stat[1, at, :]
            new_top = jnp.maximum(old_top, top)
            row_stat[0, at, :] = new_top
            row_stat[1, at, :] = old_total * jnp.exp(old_top - new_top) + total * jnp.exp(top - new_top)

    def row_copy(which, to, there):
        return pltpu.make_async_remote_copy(
            src_ref=row_stat, dst_ref=row_got.at[there],
            send_sem=rs_send.at[which], recv_sem=rs_recv.at[there],
            device_id=to, device_id_type=MESH,
        )

    start(row_copy(0, mate, 0))
    for c in (0, 1):
        start(row_copy(1 + c, downs[c], 1 + core))
        start(row_copy(3 + c, ups[c], 3 + core))

    def col_copy(by):
        return pltpu.make_async_remote_copy(
            src_ref=col_stat, dst_ref=col_got.at[z],
            send_sem=cs_send.at[by], recv_sem=cs_recv.at[by],
            device_id=device(col, ring(by), core), device_id_type=MESH,
        )

    def col_arrival(by):
        there = col_got.at[ring(-by)]
        return pltpu.make_async_remote_copy(
            src_ref=there, dst_ref=there,
            send_sem=cs_send.at[by], recv_sem=cs_recv.at[by],
            device_id=mate, device_id_type=MESH,
        )

    for by in (4, 3, 5, 2, 6, 1, 7):
        start(col_copy(by))
    col_got[z] = col_stat[...]

    for there in range(5):
        pltpu.make_async_remote_copy(
            src_ref=row_got.at[there], dst_ref=row_got.at[there],
            send_sem=rs_send.at[0], recv_sem=rs_recv.at[there],
            device_id=mate, device_id_type=MESH,
        ).wait_recv()
    for place in range(4):
        found = [(row_stat[0, place : place + 1, :], row_stat[1, place : place + 1, :])]
        others = (0, 3, 4) if place < 2 else (0, 1, 2)
        for there in others:
            row = place if there == 0 else (place + 2) % 4
            found.append((row_got[there, 0, row : row + 1, :], row_got[there, 1, row : row + 1, :]))
        top = functools.reduce(jnp.maximum, [f[0] for f in found])
        total = functools.reduce(jnp.add, [f[1] * jnp.exp(f[0] - top) for f in found])
        lse = top + jnp.log(total)
        row_lse[place : place + 1, :] = lse
        row_wide[place] = jnp.broadcast_to(lse, (ROWS, ROWS)).T

    for by in range(1, RING):
        col_arrival(by).wait_recv()
    top = functools.reduce(jnp.maximum, [col_got[i, 0] for i in range(RING)])
    total = functools.reduce(jnp.add, [col_got[i, 1] * jnp.exp(col_got[i, 0] - top) for i in range(RING)])
    hit_sum = functools.reduce(jnp.add, [col_got[i, 2] for i in range(RING)])
    col_lse[0] = top + jnp.log(total)
    col_lse[1] = hit_sum

    def weigh(step):
        height = ring(step)
        kind = abs(step) % 2
        first = lax.div(starts[kind], ROWS)
        value = scores[number(step)]
        rows = row_wide[pl.ds(first, 2)].reshape(2 * ROWS, ROWS)
        weight = 0.5 * (jnp.exp(value - rows) + jnp.exp(value - col_lse[0, pl.ds(height, 1), :]))
        if kind == 0:
            ones = jnp.where(hits(height), 1.0, 0.0)
            weight = jnp.concatenate([weight[:ROWS] - ones, weight[ROWS:]], axis=0)
        weight = weight.astype(BF16)
        weights[kind, :, pl.ds(pl.multiple_of(ROWS * lax.div(height, 2), ROWS), ROWS)] = weight
        left = images[pl.ds(first, 2)].reshape(2 * ROWS, -1)
        terms[number(step)] = dot(weight, left, ((0,), (0,)))

    def sum_copy(way, depth, half):
        to = device(col, ring(-1 if way == 0 else 1), core)
        return pltpu.make_async_remote_copy(
            src_ref=sums_out.at[way, depth - 1, half], dst_ref=sums_in.at[way, depth - 1, half],
            send_sem=sum_send.at[way, depth - 1, half], recv_sem=sum_recv.at[way, depth - 1, half],
            device_id=to, device_id_type=MESH,
        )

    def hand_on(way, depth, half, fresh):
        step = 4 if depth == 4 else (-depth if way == 0 else depth)
        value = terms[number(step), half * HALF : (half + 1) * HALF, :]
        if not fresh:
            sum_copy(way, depth + 1, half).wait_recv()
            value = value + sums_in[way, depth, half].astype(F32)
        sums_out[way, depth - 1, half] = value.astype(BF16)
        start(sum_copy(way, depth, half))

    weigh(4)
    hand_on(0, 4, 0, True)
    hand_on(1, 4, 1, True)
    weigh(-3)
    hand_on(0, 3, 1, True)
    weigh(3)
    hand_on(1, 3, 0, True)
    weigh(-2)
    weigh(2)
    hand_on(0, 3, 0, False)
    hand_on(1, 3, 1, False)
    weigh(-1)
    weigh(1)
    weigh(0)

    img_acc[...] = jnp.zeros(img_acc.shape, F32)
    for kind in (0, 1):
        parity = odd if kind == 0 else 1 - odd
        first = lax.div(starts[kind], ROWS)
        right = texts[pl.ds(4 * parity, 4)].reshape(4 * ROWS, -1)
        share = dot(weights[kind], right, ((1,), (0,)))
        img_acc[pl.ds(first, 2)] += share.reshape(2, ROWS, -1)

    img_out[0] = img_acc[1 - core].astype(BF16)
    img_out[1] = img_acc[2].astype(BF16)
    img_out[2] = img_acc[3].astype(BF16)

    def grad_copy(which, to, there):
        return pltpu.make_async_remote_copy(
            src_ref=img_out.at[which], dst_ref=img_in.at[there],
            send_sem=ig_send.at[which], recv_sem=ig_recv.at[there],
            device_id=to, device_id_type=MESH,
        )

    start(grad_copy(0, mate, 0))
    start(grad_copy(1, ups[0], 1 + core))
    start(grad_copy(2, ups[1], 1 + core))

    hand_on(0, 2, 1, False)
    hand_on(1, 2, 0, False)
    hand_on(0, 2, 0, False)
    hand_on(1, 2, 1, False)
    hand_on(0, 1, 1, False)
    hand_on(1, 1, 0, False)
    hand_on(0, 1, 0, False)
    hand_on(1, 1, 1, False)

    hit_row = jnp.sum(row_hit[...].T, axis=0, keepdims=True)
    row_ref[...] = row_lse[pl.ds(core, 1), :] - hit_row
    col_ref[...] = col_lse[0, pl.ds(z, 1), :] - col_lse[1, pl.ds(z, 1), :]

    def finish(source, summed):
        unit, inverse = unit_of(source)
        summed = factor * summed
        return (summed - unit * jnp.sum(unit * summed, axis=-1, keepdims=True)) * inverse

    for there in range(3):
        pltpu.make_async_remote_copy(
            src_ref=img_in.at[there], dst_ref=img_in.at[there],
            send_sem=ig_send.at[0], recv_sem=ig_recv.at[there],
            device_id=mate, device_id_type=MESH,
        ).wait_recv()
    igrad_ref[...] = finish(
        img_ref[...],
        img_acc[core] + img_in[0].astype(F32) + img_in[1].astype(F32) + img_in[2].astype(F32),
    )

    for turn in (0, 1):
        for way in (0, 1):
            half = 1 - turn if way == 0 else turn
            sum_copy(way, 1, half).wait_recv()
    for half in (0, 1):
        at = slice(half * HALF, (half + 1) * HALF)
        total = terms[0, at, :] + sums_in[0, 0, half].astype(F32) + sums_in[1, 0, half].astype(F32)
        tgrad_ref[at, :] = finish(txt_ref[at, :], total)

    for copy in sent:
        copy.wait_send()


def on_device(image, text, positive, logit_scale, *, columns):
    width = image.shape[1]
    vmem = pl.BlockSpec(memory_space=pltpu.VMEM)
    dma = pltpu.SemaphoreType.DMA
    row_loss, col_loss, img_grad, txt_grad = pl.pallas_call(
        functools.partial(kernel, columns),
        out_shape=(
            jax.ShapeDtypeStruct((1, ROWS), F32),
            jax.ShapeDtypeStruct((1, ROWS), F32),
            jax.ShapeDtypeStruct((ROWS, width), F32),
            jax.ShapeDtypeStruct((ROWS, width), F32),
        ),
        in_specs=[pl.BlockSpec(memory_space=pltpu.SMEM), vmem, vmem, vmem],
        out_specs=(vmem,) * 4,
        scratch_shapes=[
            pltpu.VMEM((RING, ROWS, width), BF16),
            pltpu.VMEM((4, ROWS, width), BF16),
            pltpu.VMEM((RING, 2 * ROWS, ROWS), F32),
            pltpu.VMEM((2, 2 * ROWS, 4 * ROWS), BF16),
            pltpu.VMEM((RING, ROWS, width), F32),
            pltpu.VMEM((4, ROWS, width), F32),
            pltpu.VMEM((2, 2 * ROWS, ROWS), F32),
            pltpu.VMEM((2, 2 * ROWS, ROWS), F32),
            pltpu.VMEM((ROWS, ROWS), F32),
            pltpu.VMEM((2, 8, ROWS), F32),
            pltpu.VMEM((5, 2, 8, ROWS), F32),
            pltpu.VMEM((3, 8, ROWS), F32),
            pltpu.VMEM((RING, 3, 8, ROWS), F32),
            pltpu.VMEM((8, ROWS), F32),
            pltpu.VMEM((2, 8, ROWS), F32),
            pltpu.VMEM((4, ROWS, ROWS), F32),
            pltpu.VMEM((2, 4, 2, HALF, width), BF16),
            pltpu.VMEM((2, 4, 2, HALF, width), BF16),
            pltpu.VMEM((3, ROWS, width), BF16),
            pltpu.VMEM((3, ROWS, width), BF16),
            dma((2, 4, 2)), dma((2, 4, 2)),
            dma((3,)), dma((3,)),
            dma((5,)), dma((5,)),
            dma((RING,)), dma((RING,)),
            dma((2, 4, 2)), dma((2, 4, 2)),
            dma((3,)), dma((3,)),
        ],
        compiler_params=pltpu.CompilerParams(collective_id=0, has_side_effects=True),
    )(logit_scale, image, text, positive)
    return row_loss.reshape(ROWS), col_loss.reshape(ROWS), img_grad, txt_grad


def solution(mesh):
    placed = (P(("blk", "rep"), None), P(("blk", "rep"), None), P("blk", "rep"), P())
    return jax.shard_map(
        functools.partial(on_device, columns=mesh.shape["blk"] // 4),
        mesh=mesh,
        in_specs=placed,
        out_specs=(
            P(("blk", "rep")),
            P(("blk", "rep")),
            P(("blk", "rep"), None),
            P(("blk", "rep"), None),
        ),
        check_vma=False,
    )
```

time: 167 us -> 71.7 us (0.43)
  the two profiles are of different devices: /device:TPU:128 before, /device:TPU:1 now
where the time goes in v1:
time: 71.7 us; the launch traced here: 71.5 us
  Pallas kernels  65.7 us (92%)
  local copies, waits for them, and re-layouts  4.48 us (6%)
  between operations  1.3 us (2%)
    pallas_call x1, Pallas kernels, on_device(): pl.pallas_call(functools.partial(kernel, columns), out_shape=(jax.ShapeDt...  65.7 us
    unnamed x10, local copies, waits for them, and re-layouts  4.48 us

profile of v1, /device:TPU:1, one launch (start us, length us, event | category | flops | bytes accessed | tf_op | source)
XLA Modules:
  0.0 71.5 jit_solution(6368436870063061190)
XLA Ops:
  1.3 65.7 %shard_map.75 = (f32[1,128]{1,0:T(1,128)}, f32[1,128]{1,0:T(1,128)}, f32[128,1024]{1,0:T(8,128)}, f32[128,1024]{1,0:T(8,128)}) custom-call(f32[1]{0:T(128)S(6)} %copy.12.scale_ref, bf16[128,1024]{1,0:T(8,128)(2,1)} %img_ref.1, bf16[128,1024]{1,0:T(8,128)(2,1)} %txt_ref.1, s32[1,128]{1,0:T(1,128)} %pos_ref.1), custom_call_target="tpu_custom_call" | custom-call | tf_op jit(solution)/shard_map/pallas_call | solution.py:369
  67.0 0.0 copy-start.2
  67.0 0.6 copy-done.2
  67.6 0.0 copy-start.1
  67.6 0.5 copy.13
  68.1 0.2 copy-done.1
  68.3 0.5 copy.14
  68.8 0.0 copy-start
  68.8 1.9 %copy.15 = f32[128,1024]{1,0:T(8,128)} copy(f32[128,1024]{1,0:T(8,128)} %get-tuple-element.18) | data formatting | bytes 1048576
  70.7 0.0 copy-done
  70.7 0.8 %copy.16 = f32[128,1024]{1,0:T(8,128)} copy(f32[128,1024]{1,0:T(8,128)S(1)} %copy-done) | data formatting | bytes 1048576
Async XLA Ops:
  67.0 0.6 copy-start.2
  67.6 0.7 copy-start.1
  68.8 1.9 %copy-start = (f32[128,1024]{1,0:T(8,128)S(1)}, f32[128,1024]{1,0:T(8,128)}, u32[]{:S(2)}) copy-start(f32[128,1024]{1,0:T(8,128)} %get-tuple-element.19) | copy-start | bytes 1572868

commit v2 on v0

v2 whole, which is shorter than its diff:
```python
import functools

import jax
import jax.numpy as jnp
from jax import lax
from jax.experimental import pallas as pl
from jax.experimental.pallas import tpu as pltpu
from jax.sharding import PartitionSpec as P

MESH = pl.DeviceIdType.MESH
F32 = jnp.float32
BF16 = jnp.bfloat16
ROWS = 128
HALF = 64
RING = 8
LOW = -1e30
OWN, BEHIND, NEAR, FAR = range(4)


def unit_of(values):
    widened = values.astype(F32)
    inverse = lax.rsqrt(jnp.sum(widened * widened, axis=-1, keepdims=True) + 1e-06)
    return widened * inverse, inverse


def dot(a, b, dims):
    return lax.dot_general(a, b, (dims, ((), ())), preferred_element_type=F32)


def halves(array):
    return [array[h * HALF : (h + 1) * HALF] for h in (0, 1)]


def kernel(
    columns,
    scale_ref, img_ref, txt_ref, pos_ref,
    row_ref, col_ref, igrad_ref, tgrad_ref,
    texts, images, pos_out, pos_in, scores, weights, terms, img_acc,
    peak, part, row_hit,
    row_stat, row_got, col_stat, col_got, row_lse, col_lse, row_wide,
    back_out, back_in, near_out, near_in, mate_out, mate_in, over_out, over_in, swap_out, swap_in,
    txt_send, txt_recv, pic_send, pic_recv, rs_send, rs_recv, cs_send, cs_recv,
    back_send, back_recv, near_send, near_recv, ig_send, ig_recv,
):
    blk, rep = lax.axis_index("blk"), lax.axis_index("rep")
    core = lax.rem(blk, 2)
    odd = lax.rem(lax.div(blk, 2), 2)
    col = lax.div(blk, 4)
    z = 2 * rep + odd
    tau = 1 - 2 * odd
    factor = scale_ref[0]

    def device(column, height, which):
        return (4 * column + 2 * lax.rem(height, 2) + which, lax.div(height, 2))

    def ring(by):
        return lax.rem(z + by + 2 * RING, RING)

    up, down = lax.rem(col + 1, columns), lax.rem(col + columns - 1, columns)
    pair_z, near_z, behind_z, far_z, ahead_z = (ring(s * tau) for s in (1, -1, -2, -3, 2))
    heights = (z, behind_z, near_z, far_z)
    other = 1 - core
    mate = device(col, z, other)
    pair = device(col, pair_z, core)
    near = device(col, near_z, core)
    behind = device(col, behind_z, core)
    ahead = device(col, ahead_z, core)

    def square(column):
        return [device(column, h, c) for h in (z, pair_z) for c in (core, other)]

    row_to = [(to, n) for n, to in enumerate(square(col)[1:])]
    row_to += [(to, 7 + n) for n, to in enumerate(square(up))]
    row_to += [(to, 3 + n) for n, to in enumerate(square(down))]
    col_to = [(near, 0)]
    col_to += [(device(col, ring(by), core), n) for by, n in ((3, 4), (-3, 3), (2, 2), (-2, 1))]

    barrier = pltpu.get_barrier_semaphore()
    friends = [to for to, _ in row_to + col_to]
    for friend in friends:
        pl.semaphore_signal(barrier, inc=1, device_id=friend, device_id_type=MESH)

    own_at, pair_at = 2 * odd + core, 2 * (1 - odd) + core
    firsts = (own_at, own_at, pair_at, pair_at)
    mate_own_at, mate_pair_at = 2 * odd + other, 2 * (1 - odd) + other

    img_unit, _ = unit_of(img_ref[...])
    images[own_at] = img_unit.astype(BF16)
    txt_unit, _ = unit_of(txt_ref[...])
    texts[OWN] = txt_unit.astype(BF16)
    pos_out[...] = jnp.broadcast_to(pos_ref[...].astype(F32), (8, ROWS))

    pl.semaphore_wait(barrier, len(friends))

    sent = []

    def remote(src, dst, send, recv, to):
        return pltpu.make_async_remote_copy(
            src_ref=src, dst_ref=dst, send_sem=send, recv_sem=recv, device_id=to, device_id_type=MESH
        )

    def arrival(place, send, recv):
        return remote(place, place, send, recv, mate)

    def start(copy, given=None):
        if given is None:
            copy.start()
        else:
            pl.when(given)(copy.start)
        sent.append((copy, given))

    def arrived(copy, given=None):
        if given is None:
            copy.wait_recv()
        else:
            pl.when(given)(copy.wait_recv)

    def text_copy(kind, half):
        src, dst, to = ((OWN, NEAR, near), (OWN, BEHIND, ahead), (NEAR, FAR, ahead))[kind]
        at = pl.ds(half * HALF, HALF)
        return remote(texts.at[src, at], texts.at[dst, at], txt_send.at[kind, half], txt_recv.at[kind, half], to)

    def text_arrival(kind, half):
        place = texts.at[(NEAR, BEHIND, FAR)[kind], pl.ds(half * HALF, HALF)]
        return arrival(place, txt_send.at[kind, half], txt_recv.at[kind, half])

    def image_copy(kind, src, dst, to):
        return remote(images.at[src], images.at[dst], pic_send.at[kind], pic_recv.at[kind], to)

    def image_arrival(kind, place):
        return arrival(images.at[place], pic_send.at[kind], pic_recv.at[kind])

    below = device(down, z, core)
    own_goes, pair_goes = own_at != 3, pair_at != 3
    mate_own_goes, mate_pair_goes = mate_own_at != 3, mate_pair_at != 3

    start(text_copy(0, 0))
    start(image_copy(0, own_at, own_at, pair))
    start(text_copy(0, 1))
    start(image_copy(1, own_at, own_at, mate))
    start(image_copy(3, own_at, own_at + 4, below), own_goes)
    start(text_copy(1, 0))
    start(text_copy(1, 1))
    start(remote(pos_out, pos_in, pic_send.at[7], pic_recv.at[7], pair))

    lanes = lax.broadcasted_iota(jnp.int32, (ROWS, ROWS), 1)
    peak[...] = jnp.full(peak.shape, LOW, F32)
    part[...] = jnp.zeros(part.shape, F32)
    row_hit[...] = jnp.zeros(row_hit.shape, F32)
    row_stat[0] = jnp.full((8, ROWS), LOW, F32)
    row_stat[1] = jnp.zeros((8, ROWS), F32)
    row_stat[2] = jnp.zeros((8, ROWS), F32)
    col_stat[0] = jnp.full((8, ROWS), LOW, F32)
    col_stat[1] = jnp.zeros((8, ROWS), F32)
    col_stat[2] = jnp.zeros((8, ROWS), F32)

    for half in (0, 1):
        text_arrival(0, half).wait_recv()
        start(text_copy(2, half))
    image_arrival(0, pair_at).wait_recv()
    start(image_copy(4, pair_at, pair_at + 4, below), pair_goes)
    start(image_copy(2, pair_at, pair_at, mate))
    arrival(pos_in, pic_send.at[7], pic_recv.at[7]).wait_recv()

    def column(values):
        return jnp.broadcast_to(values, (ROWS, ROWS)).T.astype(jnp.int32)

    positive = (column(pos_out[0:1, :]), column(pos_in[0:1, :]))

    image_arrival(1, mate_own_at).wait_recv()
    image_arrival(2, mate_pair_at).wait_recv()
    arrived(image_arrival(3, own_at + 4), own_goes)
    start(image_copy(5, own_at + 4, own_at + 4, mate), own_goes)
    arrived(image_arrival(4, pair_at + 4), pair_goes)
    start(image_copy(6, pair_at + 4, pair_at + 4, mate), pair_goes)
    arrived(image_arrival(5, mate_own_at + 4), mate_own_goes)
    arrived(image_arrival(6, mate_pair_at + 4), mate_pair_goes)

    def hits(which):
        return positive[which // 2] == lanes + ROWS * lax.div(heights[which], 2)

    def window(which):
        return images[pl.ds(firsts[which], 4)].reshape(4 * ROWS, -1)

    def score(which):
        value = factor * dot(window(which), texts[which], ((1,), (1,)))
        scores[which] = value
        highest = jnp.max(value, axis=0, keepdims=True)
        at = pl.ds(heights[which], 1)
        col_stat[0, at, :] = highest
        col_stat[1, at, :] = jnp.sum(jnp.exp(value - highest), axis=0, keepdims=True)
        hit = jnp.where(hits(which), value[:ROWS], 0.0)
        row_hit[which // 2] += hit
        col_stat[2, at, :] = jnp.sum(hit, axis=0, keepdims=True)
        blocks = value.reshape(4, ROWS, ROWS)
        here = pl.ds(firsts[which], 4)
        old = peak[here]
        top = jnp.maximum(old, blocks)
        part[here] = part[here] * jnp.exp(old - top) + jnp.exp(blocks - top)
        peak[here] = top

    def row_total(place):
        tops, parts = peak[place].T, part[place].T
        top = jnp.max(tops, axis=0, keepdims=True)
        row_stat[0, pl.ds(place, 1), :] = top
        row_stat[1, pl.ds(place, 1), :] = jnp.sum(parts * jnp.exp(tops - top), axis=0, keepdims=True)

    score(OWN)
    score(NEAR)
    text_arrival(1, 0).wait_recv()
    text_arrival(1, 1).wait_recv()
    score(BEHIND)
    row_total(own_at + 2 * odd)
    row_total(own_at + 2 * odd + 1)
    row_stat[2, pl.ds(own_at, 1), :] = jnp.sum(row_hit[0].T, axis=0, keepdims=True)
    text_arrival(2, 0).wait_recv()
    text_arrival(2, 1).wait_recv()
    score(FAR)
    for n in range(4):
        row_total(pair_at + n)
    row_stat[2, pl.ds(pair_at, 1), :] = jnp.sum(row_hit[1].T, axis=0, keepdims=True)

    for to, n in row_to:
        start(remote(row_stat, row_got.at[n], rs_send.at[n], rs_recv.at[n], to))
    for to, n in col_to:
        start(remote(col_stat, col_got.at[n], cs_send.at[n], cs_recv.at[n], to))

    def total_of(found):
        top = functools.reduce(jnp.maximum, [f[0] for f in found])
        return top + jnp.log(functools.reduce(jnp.add, [f[1] * jnp.exp(f[0] - top) for f in found]))

    for n in range(11):
        arrival(row_got.at[n], rs_send.at[n], rs_recv.at[n]).wait_recv()
    found = [(row_stat[0], row_stat[1])] + [(row_got[n, 0], row_got[n, 1]) for n in range(3)]
    for n in range(4):
        found.append(
            tuple(
                jnp.concatenate([row_got[7 + n, k, 4:8, :], row_got[3 + n, k, 0:4, :]], axis=0) for k in (0, 1)
            )
        )
    row_lse[...] = total_of(found)
    for n in range(6):
        row_wide[core + n] = jnp.broadcast_to(row_lse[pl.ds(core + n, 1), :], (ROWS, ROWS)).T

    for n in range(5):
        arrival(col_got.at[n], cs_send.at[n], cs_recv.at[n]).wait_recv()
    found = [(col_stat[0], col_stat[1])] + [(col_got[n, 0], col_got[n, 1]) for n in range(5)]
    col_lse[0] = total_of(found)
    col_lse[1] = functools.reduce(jnp.add, [col_stat[2]] + [col_got[n, 2] for n in range(5)])

    def weigh(which):
        value = scores[which]
        rows = row_wide[pl.ds(firsts[which], 4)].reshape(4 * ROWS, ROWS)
        weight = 0.5 * (jnp.exp(value - rows) + jnp.exp(value - col_lse[0, pl.ds(heights[which], 1), :]))
        ones = jnp.where(hits(which), 1.0, 0.0)
        weight = jnp.concatenate([weight[:ROWS] - ones, weight[ROWS:]], axis=0).astype(BF16)
        kind, side = divmod(which, 2)
        weights[kind, :, side * ROWS : (side + 1) * ROWS] = weight
        return dot(weight, window(which), ((0,), (0,)))

    def back_copy(kind, half):
        place = (kind, half)
        return remote(back_out.at[place], back_in.at[place], back_send.at[place], back_recv.at[place], behind)

    def near_copy(half):
        return remote(near_out.at[half], near_in.at[half], near_send.at[half], near_recv.at[half], near)

    for kind, which in ((1, FAR), (0, BEHIND)):
        for half, share in enumerate(halves(weigh(which))):
            back_out[kind, half] = share.astype(BF16)
            start(back_copy(kind, half))
    terms[0] = weigh(NEAR)
    terms[1] = weigh(OWN)

    img_acc[...] = jnp.zeros(img_acc.shape, F32)
    for kind, first in ((0, own_at), (1, pair_at)):
        right = texts[2 * kind : 2 * kind + 2].reshape(2 * ROWS, -1)
        img_acc[pl.ds(first, 4)] += dot(weights[kind], right, ((1,), (0,))).reshape(4, ROWS, -1)

    def grad_copy(n, src, dst, to):
        return remote(src, dst, ig_send.at[n], ig_recv.at[n], to)

    mates = [grad_copy(k, mate_out.at[k], mate_in.at[k], mate) for k in range(3)]
    for k in (2, 1, 0):
        mate_out[k] = img_acc[core + 1 + 2 * k].astype(BF16)
        start(mates[k])
    above = device(up, z, core)
    overs = [grad_copy(3 + k, over_out.at[k], over_in.at[k], above) for k in (0, 1)]
    swap = grad_copy(5, swap_out, swap_in, pair)
    for k in (2, 1, 0):
        mates[k].wait_recv()
        img_acc[2 - core + 2 * k] += mate_in[k].astype(F32)
    for k, (place, goes) in enumerate(((pair_at, pair_goes), (own_at, own_goes))):
        over_out[k] = img_acc[4 + place].astype(BF16)
        start(overs[k], goes)

    for half in (0, 1):
        back_copy(1, half).wait_recv()
        near_out[half] = (halves(terms[0])[half] + back_in[1, half].astype(F32)).astype(BF16)
        start(near_copy(half))

    for k, (place, goes) in enumerate(((pair_at, pair_goes), (own_at, own_goes))):
        @pl.when(goes)
        def _():
            overs[k].wait_recv()
            img_acc[place] += over_in[k].astype(F32)

        if k == 0:
            swap_out[...] = img_acc[pair_at].astype(BF16)
            start(swap)

    row_ref[...] = row_lse[pl.ds(own_at, 1), :] - (
        row_stat[2, pl.ds(own_at, 1), :] + row_got[1, 2, pl.ds(own_at, 1), :]
    )
    col_ref[...] = col_lse[0, pl.ds(z, 1), :] - col_lse[1, pl.ds(z, 1), :]

    def finish(source, summed):
        unit, inverse = unit_of(source)
        summed = factor * summed
        return (summed - unit * jnp.sum(unit * summed, axis=-1, keepdims=True)) * inverse

    swap.wait_recv()
    igrad_ref[...] = finish(img_ref[...], img_acc[own_at] + swap_in[...].astype(F32))

    for half in (0, 1):
        at = slice(half * HALF, (half + 1) * HALF)
        back_copy(0, half).wait_recv()
        near_copy(half).wait_recv()
        total = terms[1, at, :] + back_in[0, half].astype(F32) + near_in[half].astype(F32)
        tgrad_ref[at, :] = finish(txt_ref[at, :], total)

    for copy, given in sent:
        if given is None:
            copy.wait_send()
        else:
            pl.when(given)(copy.wait_send)


def hand_out(row_in, col_in, igrad_in, tgrad_in, row_ref, col_ref, igrad_ref, tgrad_ref, sems):
    copies = [
        pltpu.make_async_copy(igrad_in, igrad_ref, sems.at[0]),
        pltpu.make_async_copy(tgrad_in, tgrad_ref, sems.at[1]),
    ]
    for copy in copies:
        copy.start()
    row_ref[...] = row_in[0]
    col_ref[...] = col_in[0]
    for copy in copies:
        copy.wait()


def on_device(image, text, positive, logit_scale, *, columns):
    width = image.shape[1]
    vmem = pl.BlockSpec(memory_space=pltpu.VMEM)
    dma = pltpu.SemaphoreType.DMA
    line, whole = pltpu.VMEM((1, ROWS), F32), pltpu.VMEM((ROWS, width), F32)
    found = pl.pallas_call(
        functools.partial(kernel, columns),
        out_shape=(line, line, whole, whole),
        in_specs=[pl.BlockSpec(memory_space=pltpu.SMEM), vmem, vmem, vmem],
        out_specs=(vmem,) * 4,
        scratch_shapes=[
            pltpu.VMEM((4, ROWS, width), BF16),
            pltpu.VMEM((8, ROWS, width), BF16),
            pltpu.VMEM((8, ROWS), F32),
            pltpu.VMEM((8, ROWS), F32),
            pltpu.VMEM((4, 4 * ROWS, ROWS), F32),
            pltpu.VMEM((2, 4 * ROWS, 2 * ROWS), BF16),
            pltpu.VMEM((2, ROWS, width), F32),
            pltpu.VMEM((8, ROWS, width), F32),
            pltpu.VMEM((8, ROWS, ROWS), F32),
            pltpu.VMEM((8, ROWS, ROWS), F32),
            pltpu.VMEM((2, ROWS, ROWS), F32),
            pltpu.VMEM((3, 8, ROWS), F32),
            pltpu.VMEM((11, 3, 8, ROWS), F32),
            pltpu.VMEM((3, 8, ROWS), F32),
            pltpu.VMEM((5, 3, 8, ROWS), F32),
            pltpu.VMEM((8, ROWS), F32),
            pltpu.VMEM((2, 8, ROWS), F32),
            pltpu.VMEM((8, ROWS, ROWS), F32),
            pltpu.VMEM((2, 2, HALF, width), BF16),
            pltpu.VMEM((2, 2, HALF, width), BF16),
            pltpu.VMEM((2, HALF, width), BF16),
            pltpu.VMEM((2, HALF, width), BF16),
            pltpu.VMEM((3, ROWS, width), BF16),
            pltpu.VMEM((3, ROWS, width), BF16),
            pltpu.VMEM((2, ROWS, width), BF16),
            pltpu.VMEM((2, ROWS, width), BF16),
            pltpu.VMEM((ROWS, width), BF16),
            pltpu.VMEM((ROWS, width), BF16),
            dma((3, 2)), dma((3, 2)),
            dma((8,)), dma((8,)),
            dma((11,)), dma((11,)),
            dma((5,)), dma((5,)),
            dma((2, 2)), dma((2, 2)),
            dma((2,)), dma((2,)),
            dma((6,)), dma((6,)),
        ],
        compiler_params=pltpu.CompilerParams(collective_id=0, has_side_effects=True),
    )(logit_scale, image, text, positive)
    flat = jax.ShapeDtypeStruct((ROWS,), F32)
    anywhere = pl.BlockSpec(memory_space=pl.ANY)
    found = [pltpu.with_memory_space_constraint(x, pltpu.VMEM) for x in found]
    return pl.pallas_call(
        hand_out,
        out_shape=(flat, flat, *[jax.ShapeDtypeStruct((ROWS, width), F32)] * 2),
        in_specs=[vmem] * 4,
        out_specs=(vmem, vmem, anywhere, anywhere),
        scratch_shapes=[dma((2,))],
    )(*found)


def solution(mesh):
    placed = (P(("blk", "rep"), None), P(("blk", "rep"), None), P("blk", "rep"), P())
    return jax.shard_map(
        functools.partial(on_device, columns=mesh.shape["blk"] // 4),
        mesh=mesh,
        in_specs=placed,
        out_specs=(
            P(("blk", "rep")),
            P(("blk", "rep")),
            P(("blk", "rep"), None),
            P(("blk", "rep"), None),
        ),
        check_vma=False,
    )
```

time: 167 us -> 67.8 us (0.41)
  the two profiles are of different devices: /device:TPU:128 before, /device:TPU:1 now
where the time goes in v2:
time: 67.8 us; the launch traced here: 67.6 us
  Pallas kernels  66.3 us (98%)
  between operations  1.29 us (2%)
    pallas_call x1, Pallas kernels, on_device(): pl.pallas_call(functools.partial(kernel, columns), out_shape=(line, line,...  64.8 us
    pallas_call x1, Pallas kernels, on_device(): pl.pallas_call(hand_out, out_shape=(flat, flat, *[jax.ShapeDtypeStruct((R...  1.5 us

profile of v2, /device:TPU:1, one launch (start us, length us, event | category | flops | bytes accessed | tf_op | source)
XLA Modules:
  0.0 67.6 jit_solution(12804826266542932800)
XLA Ops:
  1.3 64.8 %shard_map.75 = (f32[1,128]{1,0:T(1,128)S(1)}, f32[1,128]{1,0:T(1,128)S(1)}, f32[128,1024]{1,0:T(8,128)S(1)}, f32[128,1024]{1,0:T(8,128)S(1)}) custom-call(f32[1]{0:T(128)S(6)} %copy.8.scale_ref, bf16[128,1024]{1,0:T(8,128)(2,1)} %img_ref.1, bf16[128,1024]{1,0:T(8,128)(2,1)} %txt_ref.1, s32[1,128]{1,0:T(1,128)} %pos_ref.1), custom_call_target="tpu_custom_call" | custom-call | tf_op jit(solution)/shard_map/pallas_call | solution.py:357
  66.1 1.5 %shard_map.76 = (f32[128]{0:T(128)}, f32[128]{0:T(128)}, f32[128,1024]{1,0:T(8,128)}, f32[128,1024]{1,0:T(8,128)}) custom-call(f32[1,128]{1,0:T(1,128)S(1)} %get-tuple-element.8.row_in, f32[1,128]{1,0:T(1,128)S(1)} %get-tuple-element.9.col_in, f32[128,1024]{1,0:T(8,128)S(1)} %get-tuple-element.10.igrad_in, f32[128,1024]{1,0:T(8,128)S(1)} %get-tuple-element.11.tgrad_in), custom_call_target="tpu_custom_call" | custom-call | tf_op jit(solution)/shard_map/pallas_call | solution.py:404

commit v3 on v2

--- a/solution.py
+++ b/solution.py
@@ -14,7 +14,6 @@
 HALF = 64
 RING = 8
 LOW = -1e30
-OWN, BEHIND, NEAR, FAR = range(4)
 
 
 def unit_of(values):
@@ -35,12 +34,12 @@
     columns,
     scale_ref, img_ref, txt_ref, pos_ref,
     row_ref, col_ref, igrad_ref, tgrad_ref,
-    texts, images, pos_out, pos_in, scores, weights, terms, img_acc,
+    texts, images, pos_out, pos_in, pos_wide, scores, weights, terms, img_acc,
     peak, part, row_hit,
     row_stat, row_got, col_stat, col_got, row_lse, col_lse, row_wide,
     back_out, back_in, near_out, near_in, mate_out, mate_in, over_out, over_in, swap_out, swap_in,
     txt_send, txt_recv, pic_send, pic_recv, rs_send, rs_recv, cs_send, cs_recv,
-    back_send, back_recv, near_send, near_recv, ig_send, ig_recv,
+    back_send, back_recv, near_send, near_recv, mate_send, mate_recv, over_send, over_recv, swap_send, swap_recv,
 ):
     blk, rep = lax.axis_index("blk"), lax.axis_index("rep")
     core = lax.rem(blk, 2)
@@ -58,7 +57,8 @@
 
     up, down = lax.rem(col + 1, columns), lax.rem(col + columns - 1, columns)
     pair_z, near_z, behind_z, far_z, ahead_z = (ring(s * tau) for s in (1, -1, -2, -3, 2))
-    heights = (z, behind_z, near_z, far_z)
+    OWN, BEHIND, NEAR, FAR = 2 * odd, 2 * odd + 1, 2 - 2 * odd, 3 - 2 * odd
+    is_odd = odd == 1
     other = 1 - core
     mate = device(col, z, other)
     pair = device(col, pair_z, core)
@@ -81,14 +81,10 @@
         pl.semaphore_signal(barrier, inc=1, device_id=friend, device_id_type=MESH)
 
     own_at, pair_at = 2 * odd + core, 2 * (1 - odd) + core
-    firsts = (own_at, own_at, pair_at, pair_at)
     mate_own_at, mate_pair_at = 2 * odd + other, 2 * (1 - odd) + other
 
-    img_unit, _ = unit_of(img_ref[...])
-    images[own_at] = img_unit.astype(BF16)
     txt_unit, _ = unit_of(txt_ref[...])
     texts[OWN] = txt_unit.astype(BF16)
-    pos_out[...] = jnp.broadcast_to(pos_ref[...].astype(F32), (8, ROWS))
 
     pl.semaphore_wait(barrier, len(friends))
 
@@ -116,7 +112,7 @@
             pl.when(given)(copy.wait_recv)
 
     def text_copy(kind, half):
-        src, dst, to = ((OWN, NEAR, near), (OWN, BEHIND, ahead), (NEAR, FAR, ahead))[kind]
+        src, dst, to = ((OWN, OWN, near), (OWN, BEHIND, ahead), (NEAR, FAR, ahead))[kind]
         at = pl.ds(half * HALF, HALF)
         return remote(texts.at[src, at], texts.at[dst, at], txt_send.at[kind, half], txt_recv.at[kind, half], to)
 
@@ -135,8 +131,11 @@
     mate_own_goes, mate_pair_goes = mate_own_at != 3, mate_pair_at != 3
 
     start(text_copy(0, 0))
+    start(text_copy(0, 1))
+    img_unit, _ = unit_of(img_ref[...])
+    images[own_at] = img_unit.astype(BF16)
+    pos_out[...] = jnp.broadcast_to(pos_ref[...].astype(F32), (8, ROWS))
     start(image_copy(0, own_at, own_at, pair))
-    start(text_copy(0, 1))
     start(image_copy(1, own_at, own_at, mate))
     start(image_copy(3, own_at, own_at + 4, below), own_goes)
     start(text_copy(1, 0))
@@ -165,7 +164,8 @@
     def column(values):
         return jnp.broadcast_to(values, (ROWS, ROWS)).T.astype(jnp.int32)
 
-    positive = (column(pos_out[0:1, :]), column(pos_in[0:1, :]))
+    pos_wide[odd] = column(pos_out[0:1, :])
+    pos_wide[1 - odd] = column(pos_in[0:1, :])
 
     image_arrival(1, mate_own_at).wait_recv()
     image_arrival(2, mate_pair_at).wait_recv()
@@ -176,49 +176,49 @@
     arrived(image_arrival(5, mate_own_at + 4), mate_own_goes)
     arrived(image_arrival(6, mate_pair_at + 4), mate_pair_goes)
 
-    def hits(which):
-        return positive[which // 2] == lanes + ROWS * lax.div(heights[which], 2)
-
-    def window(which):
-        return images[pl.ds(firsts[which], 4)].reshape(4 * ROWS, -1)
-
-    def score(which):
-        value = factor * dot(window(which), texts[which], ((1,), (1,)))
+    def hits(parity, height):
+        return pos_wide[parity] == lanes + ROWS * lax.div(height, 2)
+
+    def window(parity):
+        return images[pl.ds(2 * parity + core, 4)].reshape(4 * ROWS, -1)
+
+    def score(which, parity, height):
+        value = factor * dot(window(parity), texts[which], ((1,), (1,)))
         scores[which] = value
         highest = jnp.max(value, axis=0, keepdims=True)
-        at = pl.ds(heights[which], 1)
+        at = pl.ds(height, 1)
         col_stat[0, at, :] = highest
         col_stat[1, at, :] = jnp.sum(jnp.exp(value - highest), axis=0, keepdims=True)
-        hit = jnp.where(hits(which), value[:ROWS], 0.0)
-        row_hit[which // 2] += hit
+        hit = jnp.where(hits(parity, height), value[:ROWS], 0.0)
+        row_hit[parity] += hit
         col_stat[2, at, :] = jnp.sum(hit, axis=0, keepdims=True)
         blocks = value.reshape(4, ROWS, ROWS)
-        here = pl.ds(firsts[which], 4)
+        here = pl.ds(2 * parity + core, 4)
         old = peak[here]
         top = jnp.maximum(old, blocks)
         part[here] = part[here] * jnp.exp(old - top) + jnp.exp(blocks - top)
         peak[here] = top
 
     def row_total(place):
-        tops, parts = peak[place].T, part[place].T
-        top = jnp.max(tops, axis=0, keepdims=True)
+        logs = (peak[place] + jnp.log(part[place])).T
+        top = jnp.max(logs, axis=0, keepdims=True)
         row_stat[0, pl.ds(place, 1), :] = top
-        row_stat[1, pl.ds(place, 1), :] = jnp.sum(parts * jnp.exp(tops - top), axis=0, keepdims=True)
-
-    score(OWN)
-    score(NEAR)
+        row_stat[1, pl.ds(place, 1), :] = jnp.sum(jnp.exp(logs - top), axis=0, keepdims=True)
+
+    score(OWN, odd, z)
+    score(NEAR, 1 - odd, near_z)
     text_arrival(1, 0).wait_recv()
     text_arrival(1, 1).wait_recv()
-    score(BEHIND)
+    score(BEHIND, odd, behind_z)
     row_total(own_at + 2 * odd)
     row_total(own_at + 2 * odd + 1)
-    row_stat[2, pl.ds(own_at, 1), :] = jnp.sum(row_hit[0].T, axis=0, keepdims=True)
+    row_stat[2, pl.ds(own_at, 1), :] = jnp.sum(row_hit[odd].T, axis=0, keepdims=True)
     text_arrival(2, 0).wait_recv()
     text_arrival(2, 1).wait_recv()
-    score(FAR)
+    score(FAR, 1 - odd, far_z)
     for n in range(4):
         row_total(pair_at + n)
-    row_stat[2, pl.ds(pair_at, 1), :] = jnp.sum(row_hit[1].T, axis=0, keepdims=True)
+    row_stat[2, pl.ds(pair_at, 1), :] = jnp.sum(row_hit[1 - odd].T, axis=0, keepdims=True)
 
     for to, n in row_to:
         start(remote(row_stat, row_got.at[n], rs_send.at[n], rs_recv.at[n], to))
@@ -248,15 +248,22 @@
     col_lse[0] = total_of(found)
     col_lse[1] = functools.reduce(jnp.add, [col_stat[2]] + [col_got[n, 2] for n in range(5)])
 
-    def weigh(which):
-        value = scores[which]
-        rows = row_wide[pl.ds(firsts[which], 4)].reshape(4 * ROWS, ROWS)
-        weight = 0.5 * (jnp.exp(value - rows) + jnp.exp(value - col_lse[0, pl.ds(heights[which], 1), :]))
-        ones = jnp.where(hits(which), 1.0, 0.0)
+    def weigh(parity, side, height):
+        value = scores[2 * parity + side]
+        rows = row_wide[pl.ds(2 * parity + core, 4)].reshape(4 * ROWS, ROWS)
+        weight = 0.5 * (jnp.exp(value - rows) + jnp.exp(value - col_lse[0, pl.ds(height, 1), :]))
+        ones = jnp.where(hits(parity, height), 1.0, 0.0)
         weight = jnp.concatenate([weight[:ROWS] - ones, weight[ROWS:]], axis=0).astype(BF16)
-        kind, side = divmod(which, 2)
-        weights[kind, :, side * ROWS : (side + 1) * ROWS] = weight
-        return dot(weight, window(which), ((0,), (0,)))
+        weights[parity, :, side * ROWS : (side + 1) * ROWS] = weight
+
+    def text_term(parity, side):
+        weight = weights[parity, :, side * ROWS : (side + 1) * ROWS]
+        return dot(weight, window(parity), ((0,), (0,)))
+
+    def image_term(parity, part_of):
+        right = texts[2 * parity : 2 * parity + 2].reshape(2 * ROWS, -1)
+        left = weights[parity, part_of * 2 * ROWS : (part_of + 1) * 2 * ROWS, :]
+        return dot(left, right, ((1,), (0,))).reshape(2, ROWS, -1)
 
     def back_copy(kind, half):
         place = (kind, half)
@@ -265,49 +272,79 @@
     def near_copy(half):
         return remote(near_out.at[half], near_in.at[half], near_send.at[half], near_recv.at[half], near)
 
-    for kind, which in ((1, FAR), (0, BEHIND)):
-        for half, share in enumerate(halves(weigh(which))):
+    def send_back(kind, value):
+        for half, share in enumerate(halves(value)):
             back_out[kind, half] = share.astype(BF16)
             start(back_copy(kind, half))
-    terms[0] = weigh(NEAR)
-    terms[1] = weigh(OWN)
-
-    img_acc[...] = jnp.zeros(img_acc.shape, F32)
-    for kind, first in ((0, own_at), (1, pair_at)):
-        right = texts[2 * kind : 2 * kind + 2].reshape(2 * ROWS, -1)
-        img_acc[pl.ds(first, 4)] += dot(weights[kind], right, ((1,), (0,))).reshape(4, ROWS, -1)
-
-    def grad_copy(n, src, dst, to):
-        return remote(src, dst, ig_send.at[n], ig_recv.at[n], to)
-
-    mates = [grad_copy(k, mate_out.at[k], mate_in.at[k], mate) for k in range(3)]
-    for k in (2, 1, 0):
-        mate_out[k] = img_acc[core + 1 + 2 * k].astype(BF16)
-        start(mates[k])
+
     above = device(up, z, core)
-    overs = [grad_copy(3 + k, over_out.at[k], over_in.at[k], above) for k in (0, 1)]
-    swap = grad_copy(5, swap_out, swap_in, pair)
-    for k in (2, 1, 0):
-        mates[k].wait_recv()
-        img_acc[2 - core + 2 * k] += mate_in[k].astype(F32)
-    for k, (place, goes) in enumerate(((pair_at, pair_goes), (own_at, own_goes))):
-        over_out[k] = img_acc[4 + place].astype(BF16)
-        start(overs[k], goes)
-
-    for half in (0, 1):
+    above_even = device(up, z, 0)
+    core_0, core_1 = core == 0, core == 1
+
+    def mate_copy(n):
+        return remote(mate_out.at[n], mate_in.at[n], mate_send.at[n], mate_recv.at[n], mate)
+
+    def over_copy(kind, half):
+        place = (kind, half)
+        to = above if kind == 0 else above_even
+        return remote(over_out.at[place], over_in.at[place], over_send.at[place], over_recv.at[place], to)
+
+    def swap_copy(half):
+        return remote(swap_out.at[half], swap_in.at[half], swap_send.at[half], swap_recv.at[half], pair)
+
+    weigh(1 - odd, 1, far_z)
+    send_back(1, text_term(1 - odd, 1))
+    weigh(1 - odd, 0, near_z)
+    weigh(odd, 0, z)
+    weigh(odd, 1, behind_z)
+    img_acc[4:6] = image_term(1, 1)
+    img_acc[2:4] = image_term(1, 0) + image_term(0, 1)
+    mate_out[0] = img_acc[5 - 2 * core].astype(BF16)
+    start(mate_copy(0))
+    for half in (0, 1):
+        over_out[1, half] = img_acc[5, half * HALF : (half + 1) * HALF, :].astype(BF16)
+        start(over_copy(1, half), core_1 & (odd == 0))
+    mate_copy(0).wait_recv()
+    for half in (0, 1):
+        at = slice(half * HALF, (half + 1) * HALF)
+        over_out[0, half] = (img_acc[4, at, :] + mate_in[0, at, :].astype(F32)).astype(BF16)
+        start(over_copy(0, half))
+    for half in (0, 1):
+        start(over_copy(1, half), core_1 & is_odd)
+    send_back(0, text_term(odd, 1))
+    img_acc[0:2] = image_term(0, 0)
+    mate_out[1] = img_acc[1].astype(BF16)
+    start(mate_copy(1))
+    mate_out[2] = img_acc[3].astype(BF16)
+    start(mate_copy(2), core_0)
+    terms[0] = text_term(1 - odd, 0)
+    terms[1] = text_term(odd, 0)
+    mate_copy(1).wait_recv()
+    img_acc[2 - 2 * core] += mate_in[1].astype(F32)
+
+    @pl.when(core_1)
+    def _():
+        mate_copy(2).wait_recv()
+        img_acc[2] += mate_in[2].astype(F32)
+
+    def take_over(kind, half, given):
+        @pl.when(given)
+        def _():
+            over_copy(kind, half).wait_recv()
+            at = slice(half * HALF, (half + 1) * HALF)
+            img_acc[2 * kind, at, :] += over_in[kind, half].astype(F32)
+
+    for half in (0, 1):
+        take_over(0, half, is_odd)
+        take_over(1, half, core_0 & (odd == 0))
+        swap_out[half] = img_acc[2 - 2 * odd, half * HALF : (half + 1) * HALF, :].astype(BF16)
+        start(swap_copy(half))
         back_copy(1, half).wait_recv()
         near_out[half] = (halves(terms[0])[half] + back_in[1, half].astype(F32)).astype(BF16)
         start(near_copy(half))
-
-    for k, (place, goes) in enumerate(((pair_at, pair_goes), (own_at, own_goes))):
-        @pl.when(goes)
-        def _():
-            overs[k].wait_recv()
-            img_acc[place] += over_in[k].astype(F32)
-
-        if k == 0:
-            swap_out[...] = img_acc[pair_at].astype(BF16)
-            start(swap)
+    for half in (0, 1):
+        take_over(0, half, odd == 0)
+        take_over(1, half, core_0 & is_odd)
 
     row_ref[...] = row_lse[pl.ds(own_at, 1), :] - (
         row_stat[2, pl.ds(own_at, 1), :] + row_got[1, 2, pl.ds(own_at, 1), :]
@@ -319,8 +356,10 @@
         summed = factor * summed
         return (summed - unit * jnp.sum(unit * summed, axis=-1, keepdims=True)) * inverse
 
-    swap.wait_recv()
-    igrad_ref[...] = finish(img_ref[...], img_acc[own_at] + swap_in[...].astype(F32))
+    for half in (0, 1):
+        at = slice(half * HALF, (half + 1) * HALF)
+        swap_copy(half).wait_recv()
+        igrad_ref[at, :] = finish(img_ref[at, :], img_acc[2 * odd, at, :] + swap_in[half].astype(F32))
 
     for half in (0, 1):
         at = slice(half * HALF, (half + 1) * HALF)
@@ -338,8 +377,9 @@
 
 def hand_out(row_in, col_in, igrad_in, tgrad_in, row_ref, col_ref, igrad_ref, tgrad_ref, sems):
     copies = [
-        pltpu.make_async_copy(igrad_in, igrad_ref, sems.at[0]),
-        pltpu.make_async_copy(tgrad_in, tgrad_ref, sems.at[1]),
+        pltpu.make_async_copy(src.at[pl.ds(n * 16, 16)], dst.at[pl.ds(n * 16, 16)], sems.at[k, n])
+        for n in range(ROWS // 16)
+        for k, (src, dst) in enumerate(((igrad_in, igrad_ref), (tgrad_in, tgrad_ref)))
     ]
     for copy in copies:
         copy.start()
@@ -364,10 +404,11 @@
             pltpu.VMEM((8, ROWS, width), BF16),
             pltpu.VMEM((8, ROWS), F32),
             pltpu.VMEM((8, ROWS), F32),
+            pltpu.VMEM((2, ROWS, ROWS), jnp.int32),
             pltpu.VMEM((4, 4 * ROWS, ROWS), F32),
             pltpu.VMEM((2, 4 * ROWS, 2 * ROWS), BF16),
             pltpu.VMEM((2, ROWS, width), F32),
-            pltpu.VMEM((8, ROWS, width), F32),
+            pltpu.VMEM((6, ROWS, width), F32),
             pltpu.VMEM((8, ROWS, ROWS), F32),
             pltpu.VMEM((8, ROWS, ROWS), F32),
             pltpu.VMEM((2, ROWS, ROWS), F32),
@@ -384,17 +425,19 @@
             pltpu.VMEM((2, HALF, width), BF16),
             pltpu.VMEM((3, ROWS, width), BF16),
             pltpu.VMEM((3, ROWS, width), BF16),
-            pltpu.VMEM((2, ROWS, width), BF16),
-            pltpu.VMEM((2, ROWS, width), BF16),
-            pltpu.VMEM((ROWS, width), BF16),
-            pltpu.VMEM((ROWS, width), BF16),
+            pltpu.VMEM((2, 2, HALF, width), BF16),
+            pltpu.VMEM((2, 2, HALF, width), BF16),
+            pltpu.VMEM((2, HALF, width), BF16),
+            pltpu.VMEM((2, HALF, width), BF16),
             dma((3, 2)), dma((3, 2)),
             dma((8,)), dma((8,)),
             dma((11,)), dma((11,)),
             dma((5,)), dma((5,)),
             dma((2, 2)), dma((2, 2)),
             dma((2,)), dma((2,)),
-            dma((6,)), dma((6,)),
+            dma((3,)), dma((3,)),
+            dma((2, 2)), dma((2, 2)),
+            dma((2,)), dma((2,)),
         ],
         compiler_params=pltpu.CompilerParams(collective_id=0, has_side_effects=True),
     )(logit_scale, image, text, positive)
@@ -406,7 +449,7 @@
         out_shape=(flat, flat, *[jax.ShapeDtypeStruct((ROWS, width), F32)] * 2),
         in_specs=[vmem] * 4,
         out_specs=(vmem, vmem, anywhere, anywhere),
-        scratch_shapes=[dma((2,))],
+        scratch_shapes=[dma((2, ROWS // 16))],
     )(*found)
 
 

time: 67.8 us -> 64.6 us (0.953)
  Pallas kernels: 66.3 us -> 63.2 us
    pallas_call x1, Pallas kernels: 64.8 us -> 61.6 us  [on_device(): pl.pallas_call(functools.partial(kernel, columns), out_shape=(line, line,...]
where the time goes in v3:
time: 64.6 us; the launch traced here: 64.5 us
  Pallas kernels  63.2 us (98%)
  between operations  1.29 us (2%)
    pallas_call x1, Pallas kernels, on_device(): pl.pallas_call(functools.partial(kernel, columns), out_shape=(line, line,...  61.6 us
    pallas_call x1, Pallas kernels, on_device(): pl.pallas_call(hand_out, out_shape=(flat, flat, *[jax.ShapeDtypeStruct((R...  1.6 us

profile of v3, /device:TPU:1, one launch (start us, length us, event | category | flops | bytes accessed | tf_op | source)
XLA Modules:
  0.0 64.5 jit_solution(276074170396372204)
XLA Ops:
  1.3 61.6 %shard_map.75 = (f32[1,128]{1,0:T(1,128)S(1)}, f32[1,128]{1,0:T(1,128)S(1)}, f32[128,1024]{1,0:T(8,128)S(1)}, f32[128,1024]{1,0:T(8,128)S(1)}) custom-call(f32[1]{0:T(128)S(6)} %copy.8.scale_ref, bf16[128,1024]{1,0:T(8,128)(2,1)} %img_ref.1, bf16[128,1024]{1,0:T(8,128)(2,1)} %txt_ref.1, s32[1,128]{1,0:T(1,128)} %pos_ref.1), custom_call_target="tpu_custom_call" | custom-call | tf_op jit(solution)/shard_map/pallas_call | solution.py:397
  62.9 1.6 %shard_map.76 = (f32[128]{0:T(128)}, f32[128]{0:T(128)}, f32[128,1024]{1,0:T(8,128)}, f32[128,1024]{1,0:T(8,128)}) custom-call(f32[1,128]{1,0:T(1,128)S(1)} %get-tuple-element.8.row_in, f32[1,128]{1,0:T(1,128)S(1)} %get-tuple-element.9.col_in, f32[128,1024]{1,0:T(8,128)S(1)} %get-tuple-element.10.igrad_in, f32[128,1024]{1,0:T(8,128)S(1)} %get-tuple-element.11.tgrad_in), custom_call_target="tpu_custom_call" | custom-call | tf_op jit(solution)/shard_map/pallas_call | solution.py:447

commit v4 on v3

--- a/solution.py
+++ b/solution.py
@@ -34,7 +34,7 @@
     columns,
     scale_ref, img_ref, txt_ref, pos_ref,
     row_ref, col_ref, igrad_ref, tgrad_ref,
-    texts, images, pos_out, pos_in, pos_wide, scores, weights, terms, img_acc,
+    units, inverses, texts, images, pos_out, pos_in, pos_wide, scores, weights, terms, img_acc,
     peak, part, row_hit,
     row_stat, row_got, col_stat, col_got, row_lse, col_lse, row_wide,
     back_out, back_in, near_out, near_in, mate_out, mate_in, over_out, over_in, swap_out, swap_in,
@@ -47,7 +47,7 @@
     col = lax.div(blk, 4)
     z = 2 * rep + odd
     tau = 1 - 2 * odd
-    factor = scale_ref[0]
+    factor = scale_ref[...]
 
     def device(column, height, which):
         return (4 * column + 2 * lax.rem(height, 2) + which, lax.div(height, 2))
@@ -142,6 +142,10 @@
     start(text_copy(1, 1))
     start(remote(pos_out, pos_in, pic_send.at[7], pic_recv.at[7], pair))
 
+    for kind, source in enumerate((img_ref, txt_ref)):
+        unit, inverse = unit_of(source[...])
+        units[kind] = unit
+        inverses[kind] = jnp.broadcast_to(inverse, (ROWS, ROWS))
     lanes = lax.broadcasted_iota(jnp.int32, (ROWS, ROWS), 1)
     peak[...] = jnp.full(peak.shape, LOW, F32)
     part[...] = jnp.zeros(part.shape, F32)
@@ -220,10 +224,12 @@
         row_total(pair_at + n)
     row_stat[2, pl.ds(pair_at, 1), :] = jnp.sum(row_hit[1 - odd].T, axis=0, keepdims=True)
 
-    for to, n in row_to:
+    for to, n in row_to[3:]:
         start(remote(row_stat, row_got.at[n], rs_send.at[n], rs_recv.at[n], to))
-    for to, n in col_to:
+    for to, n in col_to[1:] + col_to[:1]:
         start(remote(col_stat, col_got.at[n], cs_send.at[n], cs_recv.at[n], to))
+    for to, n in row_to[:3]:
+        start(remote(row_stat, row_got.at[n], rs_send.at[n], rs_recv.at[n], to))
 
     def total_of(found):
         top = functools.reduce(jnp.maximum, [f[0] for f in found])
@@ -351,22 +357,23 @@
     )
     col_ref[...] = col_lse[0, pl.ds(z, 1), :] - col_lse[1, pl.ds(z, 1), :]
 
-    def finish(source, summed):
-        unit, inverse = unit_of(source)
+    def finish(kind, at, summed):
+        unit = units[kind, at, :]
         summed = factor * summed
-        return (summed - unit * jnp.sum(unit * summed, axis=-1, keepdims=True)) * inverse
+        return (summed - unit * jnp.sum(unit * summed, axis=-1, keepdims=True)) * inverses[kind, at, 0:1]
 
     for half in (0, 1):
         at = slice(half * HALF, (half + 1) * HALF)
         swap_copy(half).wait_recv()
-        igrad_ref[at, :] = finish(img_ref[at, :], img_acc[2 * odd, at, :] + swap_in[half].astype(F32))
+        igrad_ref[at, :] = finish(0, at, img_acc[2 * odd, at, :] + swap_in[half].astype(F32))
 
     for half in (0, 1):
         at = slice(half * HALF, (half + 1) * HALF)
         back_copy(0, half).wait_recv()
+        total = terms[1, at, :] + back_in[0, half].astype(F32)
         near_copy(half).wait_recv()
-        total = terms[1, at, :] + back_in[0, half].astype(F32) + near_in[half].astype(F32)
-        tgrad_ref[at, :] = finish(txt_ref[at, :], total)
+        total += near_in[half].astype(F32)
+        tgrad_ref[at, :] = finish(1, at, total)
 
     for copy, given in sent:
         if given is None:
@@ -397,9 +404,11 @@
     found = pl.pallas_call(
         functools.partial(kernel, columns),
         out_shape=(line, line, whole, whole),
-        in_specs=[pl.BlockSpec(memory_space=pltpu.SMEM), vmem, vmem, vmem],
+        in_specs=[vmem] * 4,
         out_specs=(vmem,) * 4,
         scratch_shapes=[
+            pltpu.VMEM((2, ROWS, width), F32),
+            pltpu.VMEM((2, ROWS, ROWS), F32),
             pltpu.VMEM((4, ROWS, width), BF16),
             pltpu.VMEM((8, ROWS, width), BF16),
             pltpu.VMEM((8, ROWS), F32),
@@ -440,7 +449,7 @@
             dma((2,)), dma((2,)),
         ],
         compiler_params=pltpu.CompilerParams(collective_id=0, has_side_effects=True),
-    )(logit_scale, image, text, positive)
+    )(logit_scale.reshape(1, 1), image, text, positive)
     flat = jax.ShapeDtypeStruct((ROWS,), F32)
     anywhere = pl.BlockSpec(memory_space=pl.ANY)
     found = [pltpu.with_memory_space_constraint(x, pltpu.VMEM) for x in found]

time: 64.6 us -> 64.5 us (level)
  no operation moved by 1% of the time
where the time goes in v4:
time: 64.5 us; the launch traced here: 64.4 us
  Pallas kernels  63.1 us (98%)
  between operations  1.29 us (2%)
    pallas_call x1, Pallas kernels, on_device(): pl.pallas_call(functools.partial(kernel, columns), out_shape=(line, line,...  61.5 us
    pallas_call x1, Pallas kernels, on_device(): pl.pallas_call(hand_out, out_shape=(flat, flat, *[jax.ShapeDtypeStruct((R...  1.6 us

profile of v4, /device:TPU:1, one launch (start us, length us, event | category | flops | bytes accessed | tf_op | source)
XLA Modules:
  0.0 64.4 jit_solution(14054686017341452232)
XLA Ops:
  1.3 61.5 %shard_map.75 = (f32[1,128]{1,0:T(1,128)S(1)}, f32[1,128]{1,0:T(1,128)S(1)}, f32[128,1024]{1,0:T(8,128)S(1)}, f32[128,1024]{1,0:T(8,128)S(1)}) custom-call(f32[1,1]{1,0:T(1,128)} %bitcast.1.scale_ref, bf16[128,1024]{1,0:T(8,128)(2,1)} %img_ref.1, bf16[128,1024]{1,0:T(8,128)(2,1)} %txt_ref.1, s32[1,128]{1,0:T(1,128)} %pos_ref.1), custom_call_target="tpu_custom_call" | custom-call | tf_op jit(solution)/shard_map/pallas_call | solution.py:404
  62.8 1.6 %shard_map.76 = (f32[128]{0:T(128)}, f32[128]{0:T(128)}, f32[128,1024]{1,0:T(8,128)}, f32[128,1024]{1,0:T(8,128)}) custom-call(f32[1,128]{1,0:T(1,128)S(1)} %get-tuple-element.8.row_in, f32[1,128]{1,0:T(1,128)S(1)} %get-tuple-element.9.col_in, f32[128,1024]{1,0:T(8,128)S(1)} %get-tuple-element.10.igrad_in, f32[128,1024]{1,0:T(8,128)S(1)} %get-tuple-element.11.tgrad_in), custom_call_target="tpu_custom_call" | custom-call | tf_op jit(solution)/shard_map/pallas_call | solution.py:456
